TPU v7x, 128 devices: a whole 4x4x4 slice. The times are simulated.
128 devices in a mesh: ctx: 8 (over y, core), fsdp: 16 (over x, z).
Axes of the slice: x: 4, y: 4, z: 4, core: 2. Of those that a mesh axis runs over, the one named last changes fastest.
Arguments:
- hidden: bfloat16 [8, 16, 256, 2048], P('ctx', 'fsdp'), may hold values from -4.5 to 4.5
- norm_gain: float32 [2048], replicated, may hold values from 0.1 to 1.9
- w_query: bfloat16 [2048, 2048], P('fsdp', 'ctx'), may hold values from -1 to 1
- w_key: bfloat16 [2048, 1024], P('fsdp', 'ctx'), may hold values from -1 to 1
- w_value: bfloat16 [2048, 1024], P('fsdp', 'ctx'), may hold values from -0.125 to 0.125
- q_gain: float32 [128], replicated, may hold values from 0.5 to 5
- k_gain: float32 [128], replicated, may hold values from 0.5 to 5
- lengths: int32 [16, 4], replicated, may hold values from 1 to 1024, 2048 in all within a row
- piece_map: int32 [16, 8], replicated, may hold values from 0 to 7, each once within a row
- owner: int32 [8, 16, 256], P('ctx', 'fsdp'), may hold values from 0 to 127, as said below
- slot: int32 [8, 16, 256], P('ctx', 'fsdp'), may hold values from 0 to 511, as said below
Outputs:
- attended: bfloat16 [8, 16, 256, 2048], P('ctx', 'fsdp')
- cache: bfloat16 [65536, 2048], P(('ctx', 'fsdp'))
Inputs may be any that keep to these rules, and one draw needn't show every extreme that they name: `lengths`: each row sums to 2048; its largest entry is 1024. `piece_map`: each row holds every piece once. At most 4 tokens of one device go to one owner; in every draw one owner receives exactly 4 from every device. `slot`: tokens with the same owner have distinct slots.
All inputs are finite; a program needn't handle non-finite values.
Results may differ from a plain program's by a relative error of at most 0.0035.
The roundings to bfloat16 on the way count: a program that leaves them out, or rounds other values in their place, can miss the bound.
Values may be sent and summed in bfloat16 or wider, within the bound.
No kernel may reach another device: no remote copies, remote signals or barrier semaphores. Data moves between devices by JAX's collectives and lax.ppermute only.
A program may use at most 128 MiB of HBM per device.

v0:
```python
import math

import jax
import jax.numpy as jnp
from jax import lax
from jax.sharding import PartitionSpec as P

HEAD_WIDTH = 128


EPSILON = 1e-06
THETA = 1000000.0
NEG_BIG = -1e30


def norm_rope(projected, gain_vec, relative, head_size):
    row_count = projected.shape[0]
    head_count = projected.shape[1] // head_size
    shaped = projected.reshape(row_count, head_count, head_size)
    factor = lax.rsqrt(jnp.mean(shaped * shaped, axis=-1, keepdims=True) + EPSILON)
    normal = shaped * factor * gain_vec
    half_size = head_size // 2
    frequency = jnp.exp(
        jnp.arange(half_size, dtype=jnp.float32) * (-2.0 * math.log(THETA) / head_size)
    )
    angles = relative.astype(jnp.float32)[:, None] * frequency[None, :]
    cosine = jnp.cos(angles)[:, None, :]
    sine_part = jnp.sin(angles)[:, None, :]
    first_half = normal[..., :half_size]
    second = normal[..., half_size:]
    turned = jnp.concatenate(
        [first_half * cosine - second * sine_part, second * cosine + first_half * sine_part],
        axis=-1,
    )
    return turned.reshape(row_count, head_count * head_size).astype(jnp.bfloat16)


def attend_keys(
    state_tuple, heads_of_query, query_pos, query_seg, key_rows, value_rows, key_pos, key_seg
):
    row_max, row_sum, weighted = state_tuple
    heads_of_key = key_rows.reshape(key_rows.shape[0], -1, HEAD_WIDTH)
    heads_of_value = value_rows.reshape(value_rows.shape[0], -1, HEAD_WIDTH)
    scores = jnp.einsum(
        "tkgd,skd->tkgs", heads_of_query, heads_of_key, preferred_element_type=jnp.float32
    ) * (1.0 / math.sqrt(HEAD_WIDTH))
    visible = ((query_seg[:, None] == key_seg[None, :]) & (key_pos[None, :] <= query_pos[:, None]))[
        :, None, None, :
    ]
    masked = jnp.where(visible, scores, NEG_BIG)
    new_max = jnp.maximum(row_max, jnp.max(masked, axis=-1))
    weights = jnp.where(visible, jnp.exp(masked - new_max[..., None]), 0.0)
    shrink = jnp.exp(row_max - new_max)
    row_sum = row_sum * shrink + jnp.sum(weights, axis=-1)
    weighted = weighted * shrink[..., None] + jnp.einsum(
        "tkgs,skd->tkgd",
        weights.astype(jnp.bfloat16),
        heads_of_value,
        preferred_element_type=jnp.float32,
    )
    return (new_max, row_sum, weighted)


def sweep_keys(
    state_tuple, heads_of_query, query_pos, query_seg, key_rows, value_rows, key_pos, key_seg
):
    row_span = key_rows.shape[0]
    key_block = 512
    steps_count = row_span // key_block

    def step_keys(carried, key_items):
        return (
            attend_keys(
                carried,
                heads_of_query,
                query_pos,
                query_seg,
                key_items[0],
                key_items[1],
                key_items[2],
                key_items[3],
            ),
            None,
        )

    result_carry, unused = lax.scan(
        step_keys,
        state_tuple,
        (
            key_rows.reshape(steps_count, key_block, -1),
            value_rows.reshape(steps_count, key_block, -1),
            key_pos.reshape(steps_count, key_block),
            key_seg.reshape(steps_count, key_block),
        ),
    )
    return result_carry


def empty_state(row_count, kv_heads, group_width):
    return (
        jnp.full((row_count, kv_heads, group_width), NEG_BIG, jnp.float32),
        jnp.zeros((row_count, kv_heads, group_width), jnp.float32),
        jnp.zeros((row_count, kv_heads, group_width, HEAD_WIDTH), jnp.float32),
    )


def project_rows(source, pieces):
    return tuple(
        (jnp.dot(source, shard_rows, preferred_element_type=jnp.float32) for shard_rows in pieces)
    )


def shards(
    hidden, norm_gain, w_query, w_key, w_value, q_gain, k_gain, lengths, piece_map, owner, slot
):
    tok_rows = hidden.shape[2]
    ctx_count = lax.axis_size("ctx")
    fsdp_count = lax.axis_size("fsdp")
    owner_count = ctx_count * fsdp_count
    group_index = lax.axis_index("fsdp")
    ctx_index = lax.axis_index("ctx")
    inputs = hidden[0, 0].astype(jnp.float32)
    factor = lax.rsqrt(jnp.mean(inputs * inputs, axis=-1, keepdims=True) + EPSILON)
    normed = (inputs * factor * norm_gain).astype(jnp.bfloat16)
    my_lengths = lax.dynamic_index_in_dim(lengths, group_index, 0, keepdims=False)
    my_pieces = lax.dynamic_index_in_dim(piece_map, group_index, 0, keepdims=False)
    seg_ends = jnp.cumsum(my_lengths, dtype=jnp.int32)
    starts = seg_ends - my_lengths
    seg_count = lengths.shape[1]

    def stream_info(row_ids):
        holder = row_ids // tok_rows
        piece_ids = jnp.sum(
            jnp.where(
                holder[:, None] == jnp.arange(ctx_count, dtype=jnp.int32)[None, :],
                my_pieces[None, :],
                0,
            ),
            axis=1,
            dtype=jnp.int32,
        )
        positions = piece_ids * tok_rows + row_ids % tok_rows
        segment = jnp.sum(
            (positions[:, None] >= seg_ends[None, :]).astype(jnp.int32), axis=1, dtype=jnp.int32
        )
        relative = positions - jnp.sum(
            jnp.where(
                segment[:, None] == jnp.arange(seg_count, dtype=jnp.int32)[None, :],
                starts[None, :],
                0,
            ),
            axis=1,
            dtype=jnp.int32,
        )
        return (positions, segment, relative)

    query_cols, key_cols, value_cols = (
        lax.all_gather(w_query, "ctx", axis=1, tiled=True),
        lax.all_gather(w_key, "ctx", axis=1, tiled=True),
        lax.all_gather(w_value, "ctx", axis=1, tiled=True),
    )
    query_raw, key_raw, value_raw = project_rows(
        normed,
        (
            lax.all_gather(query_cols, "fsdp", axis=0, tiled=True),
            lax.all_gather(key_cols, "fsdp", axis=0, tiled=True),
            lax.all_gather(value_cols, "fsdp", axis=0, tiled=True),
        ),
    )
    own_ids = ctx_index * tok_rows + jnp.arange(tok_rows, dtype=jnp.int32)
    own_pos, own_seg, own_rel = stream_info(own_ids)
    query_rows = norm_rope(query_raw, q_gain, own_rel, HEAD_WIDTH)
    key_new = norm_rope(key_raw, k_gain, own_rel, HEAD_WIDTH)
    value_new = value_raw.astype(jnp.bfloat16)
    kv_heads = key_new.shape[1] // HEAD_WIDTH
    group_width = query_rows.shape[1] // key_new.shape[1]
    heads_of_query = query_rows.reshape(tok_rows, kv_heads, group_width, HEAD_WIDTH)
    pieces = (
        lax.all_gather(key_new, "ctx", axis=0, tiled=True),
        lax.all_gather(value_new, "ctx", axis=0, tiled=True),
    )
    row_ids = jnp.arange(pieces[0].shape[0], dtype=jnp.int32)
    key_pos, key_seg, unused = stream_info(row_ids)
    row_max, row_sum, weighted = sweep_keys(
        empty_state(tok_rows, kv_heads, group_width),
        heads_of_query,
        own_pos,
        own_seg,
        pieces[0],
        pieces[1],
        key_pos,
        key_seg,
    )
    attended = (weighted / row_sum[..., None]).reshape(tok_rows, -1).astype(jnp.bfloat16)
    kv_new = jnp.concatenate([key_new, value_new], axis=1)
    kv_width = kv_new.shape[1]
    per_owner = 2 * tok_rows // owner_count
    capacity = owner_count * per_owner
    own_owner = owner[0, 0]
    own_slot = slot[0, 0]
    onehot = (own_owner[:, None] == jnp.arange(owner_count, dtype=jnp.int32)[None, :]).astype(
        jnp.int32
    )
    rank_in_owner = jnp.sum(
        onehot * (jnp.cumsum(onehot, axis=0, dtype=jnp.int32) - 1), axis=1, dtype=jnp.int32
    )
    bucket_pos = own_owner * per_owner + rank_in_owner
    bucket = jnp.zeros((capacity, kv_width), jnp.bfloat16).at[bucket_pos].set(kv_new)
    bucket_slots = jnp.full((capacity,), capacity, jnp.int32).at[bucket_pos].set(own_slot)
    got_rows, got_slots = (
        lax.all_to_all(
            bucket.reshape(owner_count, per_owner, kv_width),
            ("ctx", "fsdp"),
            split_axis=0,
            concat_axis=0,
            tiled=True,
        ),
        lax.all_to_all(
            bucket_slots.reshape(owner_count, per_owner),
            ("ctx", "fsdp"),
            split_axis=0,
            concat_axis=0,
            tiled=True,
        ),
    )
    new_cache = (
        jnp.zeros((capacity, kv_width), jnp.bfloat16)
        .at[got_slots.reshape(-1)]
        .set(got_rows.reshape(-1, kv_width), mode="drop")
    )
    return (attended[None, None], new_cache)


def solution(mesh):
    placed = (
        P("ctx", "fsdp", None, None),
        P(),
        P("fsdp", "ctx"),
        P("fsdp", "ctx"),
        P("fsdp", "ctx"),
        P(),
        P(),
        P(),
        P(),
        P("ctx", "fsdp", None),
        P("ctx", "fsdp", None),
    )
    return jax.shard_map(
        shards,
        mesh=mesh,
        in_specs=placed,
        out_specs=(P("ctx", "fsdp", None, None), P(("ctx", "fsdp"), None)),
        check_vma=False,
    )
```

profile of v0, /device:TPU:1, one launch (start us, length us, event | category | flops | bytes accessed | tf_op | source)
XLA Modules:
  0.0 381.6 jit_solution(15677622843119619807)
XLA Ops:
  7.2 15.2 %all_gather.24 = bf16[128,1024]{1,0:T(8,128)(2,1)} all-gather(bf16[128,128]{1,0:T(8,128)(2,1)} %param.16), channel_id=1, replica_groups=mesh['ctx'=8,'fsdp'=16] {'ctx'}, dimensions={1}, use_global_device_ids=true | all-gather | bytes 294912 | tf_op jit(solution)/shard_map/all_gather | solution.py:159
  22.5 12.6 %all_gather.29 = bf16[128,1024]{1,0:T(8,128)(2,1)} all-gather(bf16[128,128]{1,0:T(8,128)(2,1)} %param.17), channel_id=1, replica_groups=mesh['ctx'=8,'fsdp'=16] {'ctx'}, dimensions={1}, use_global_device_ids=true | all-gather | bytes 294912 | tf_op jit(solution)/shard_map/all_gather | solution.py:160
  35.2 14.4 %all_gather.27 = bf16[128,2048]{1,0:T(8,128)(2,1)} all-gather(bf16[128,256]{1,0:T(8,128)(2,1)} %param.15), channel_id=1, replica_groups=mesh['ctx'=8,'fsdp'=16] {'ctx'}, dimensions={1}, use_global_device_ids=true | all-gather | bytes 589824 | tf_op jit(solution)/shard_map/all_gather | solution.py:158
  51.1 23.9 %all-gather.6.cloned.1.call-done = bf16[2048,1024]{1,0:T(8,128)(2,1)} async-done(((bf16[128,1024]{1,0:T(8,128)(2,1)}), bf16[2048,1024]{1,0:T(8,128)(2,1)}) %all-gather.6.cloned.1.call-update) | async-done | bytes 4194320 | tf_op jit(solution)/shard_map/all_gather | solution.py:166
  75.0 6.5 %copy.64 = bf16[1024,2048]{1,0:T(8,128)(2,1)} copy(bf16[1024,2048]{0,1:T(8,128)(2,1)} %bitcast.121) | data formatting | bytes 8388608 | tf_op jit(solution)/shard_map/dot_general | solution.py:109
  81.5 3.6 multiply_reduce_fusion.1
  85.6 1.0 copy.65
  86.7 41.8 %all-gather.12.cloned.1.call-done = bf16[2048,1024]{1,0:T(8,128)(2,1)} async-done(((bf16[128,1024]{1,0:T(8,128)(2,1)}), bf16[2048,1024]{1,0:T(8,128)(2,1)}) %all-gather.12.cloned.1.call-update) | async-done | bytes 4194320 | tf_op jit(solution)/shard_map/all_gather | solution.py:167
  128.4 4.3 %convolution_convert_fusion = bf16[256,1024]{1,0:T(8,128)(2,1)} fusion(bf16[2048,1024]{1,0:T(8,128)(2,1)} %all-gather.12.cloned.1.call-done, bf16[1,1,256,2048]{3,2,1,0:T(8,128)(2,1)S(1)} %copy-done.3, f32[2048]{0:T(1024)S(1)} %copy-done.9, f32[256]{0:T(256)S(1)} %add_rsqrt_fusion.2), kind=kOutput, calls=%fused_computation.37 | convolution fusion | flops 1076101120 | bytes 5776384 | tf_op jit(solution)/shard_map/dot_general | solution.py:109
  133.4 1.6 scatter_custom_fusion
  135.0 0.7 all_to_all.9
  135.7 7.9 %all-to-all-start = ((s32[128,1,4]{2,1,0:T(1,128)}), s32[128,1,4]{2,1,0:T(1,128)S(1)}, u32[]{:S(2)}, u32[]{:S(2)}) async-start(s32[128,1,4]{2,1,0:T(1,128)} %bitcast.26), calls=%async_computation | async-start | bytes 131072 | tf_op jit(solution)/shard_map/all_to_all | solution.py:218
  143.6 3.3 scatter_custom_fusion.1
  146.9 2.2 reshape.385
  149.1 4.1 %all-to-all-done = s32[128,1,4]{2,1,0:T(1,128)S(1)} async-done(((s32[128,1,4]{2,1,0:T(1,128)}), s32[128,1,4]{2,1,0:T(1,128)S(1)}, u32[]{:S(2)}, u32[]{:S(2)}) %all-to-all-start) | async-done | bytes 2080 | tf_op jit(solution)/shard_map/all_to_all | solution.py:218
  153.2 5.7 %all-to-all-start.1 = ((bf16[128,4,2048]{2,1,0:T(4,128)(2,1)}), bf16[128,4,2048]{2,1,0:T(4,128)(2,1)S(1)}, u32[]{:S(2)}, u32[]{:S(2)}) async-start(bf16[128,4,2048]{2,1,0:T(4,128)(2,1)} %reshape.385), calls=%async_computation.1 | async-start | bytes 4194304 | tf_op jit(solution)/shard_map/all_to_all | solution.py:211
  159.7 0.8 reduce.5
  160.7 45.7 %all-to-all-done.1 = bf16[128,4,2048]{2,1,0:T(4,128)(2,1)S(1)} async-done(((bf16[128,4,2048]{2,1,0:T(4,128)(2,1)}), bf16[128,4,2048]{2,1,0:T(4,128)(2,1)S(1)}, u32[]{:S(2)}, u32[]{:S(2)}) %all-to-all-start.1) | async-done | bytes 2097184 | tf_op jit(solution)/shard_map/all_to_all | solution.py:211
  206.4 2.1 reshape.408
  208.4 6.2 %scatter_custom_fusion.2 = bf16[512,2048]{1,0:T(8,128)(2,1)} fusion(s32[512]{0:T(512)S(1)} %bitcast.132, bf16[512,2048]{1,0:T(8,128)(2,1)} %reshape.408, bf16[]{:T(256)} %constant.129.clone.1), kind=kCustom, calls=%fused_computation.44 | custom fusion | bytes 2097664 | tf_op jit(solution)/shard_map/scatter | solution.py:229
  214.7 5.5 %all-gather.10.cloned.1.call-done = bf16[2048,2048]{1,0:T(8,128)(2,1)} async-done(((bf16[128,2048]{1,0:T(8,128)(2,1)}), bf16[2048,2048]{1,0:T(8,128)(2,1)}) %all-gather.10.cloned.1.call-update) | async-done | bytes 8388624 | tf_op jit(solution)/shard_map/all_gather | solution.py:165
  220.1 12.5 %copy.66 = bf16[2048,2048]{1,0:T(8,128)(2,1)} copy(bf16[2048,2048]{0,1:T(8,128)(2,1)} %bitcast.116) | data formatting | bytes 16777216 | tf_op jit(solution)/shard_map/dot_general | solution.py:109
  232.6 6.0 %multiply_reduce_fusion = (f32[256,16]{0,1:T(8,128)S(1)}, f32[256,16,128]{0,2,1:T(8,128)S(1)}) fusion(bf16[16,128,2048]{2,1,0:T(8,128)(2,1)} %bitcast.117, bf16[1,1,256,2048]{3,2,1,0:T(8,128)(2,1)S(1)} %copy-done.4, f32[2048]{0:T(1024)S(1)} %copy-done.9, f32[256]{0:T(256)S(1)} %add_rsqrt_fusion.2), kind=kOutput, calls=%fused_computation.36 | convolution fusion | flops 2150625280 | bytes 11559936 | tf_op jit(solution)/shard_map/dot_general | solution.py:109
  239.4 1.3 copy.68
  240.7 12.2 %all-gather.8.cloned.1.call-done = bf16[2048,1024]{1,0:T(8,128)(2,1)} async-done(((bf16[256,1024]{1,0:T(8,128)(2,1)}), bf16[2048,1024]{1,0:T(8,128)(2,1)}) %all-gather.8.cloned.1.call-update) | async-done | bytes 4194320 | tf_op jit(solution)/shard_map/all_gather | solution.py:179
  253.0 33.7 %all-gather.14.cloned.1.call-done = bf16[2048,1024]{1,0:T(8,128)(2,1)} async-done(((bf16[256,1024]{1,0:T(8,128)(2,1)}), bf16[2048,1024]{1,0:T(8,128)(2,1)}) %all-gather.14.cloned.1.call-update) | async-done | bytes 4194320 | tf_op jit(solution)/shard_map/all_gather | solution.py:180
  286.6 85.2 %while.15 = (s32[]{:T(128)}, f32[256,8,2]{0,2,1:T(2,128)S(1)}, f32[256,8,2]{0,2,1:T(2,128)S(1)}, f32[256,8,2,128]{0,3,2,1:T(8,128)}, s32[256]{0:T(256)S(1)}, /*i...) while((s32[]{:T(128)}, f32[256,8,2]{0,2,1:T(2,128)S(1)}, ...), condition=%wide.region_12.13_spmd.clone, body=%wide.region_9.12_spmd.clone.sunk | while | flops 1102991360 | bytes 41695372 | solution.py:86
  286.8 1.7 constant_dynamic-slice_fusion.8
  288.6 0.5 copy.86
  289.1 6.0 %fusion.72 = (f32[256,8,2]{0,2,1:T(2,128)S(1)}, f32[8,512,256,2]{2,1,3,0:T(8,128)}) fusion(pred[256,512]{0,1:T(8,128)(4,1)S(1)} %compare_and_fusion.2, bf16[512,8,128,1]{0,2,3,1:T(8,128)(2,1)S(1)} %bitcast.114, bf16[256,8,2,128]{3,0,2,1:T(8,128)(2,1)} %get-tuple-element.313), kind=kOutput, calls=%fused_computation.5.clone.1 | convolution fusion | flops 543158272 | bytes 10633216 | tf_op jit(solution)/shard_map/while/body/eval_jaxpr/tkgd,skd->tkgs/dot_general | solution.py:44
  295.2 4.5 %fusion.74 = f32[256,8,2]{0,2,1:T(2,128)S(1)} fusion(f32[8,512,256,2]{2,1,3,0:T(8,128)} %get-tuple-element.274, f32[256,8,2]{0,2,1:T(2,128)S(1)} %fusion.73, pred[256,512]{0,1:T(8,128)(4,1)S(1)} %compare_and_fusion.2), kind=kLoop, calls=%fused_computation.7.clone.1 | loop fusion | flops 10481664 | bytes 8552448 | tf_op jit(solution)/shard_map/while/body/eval_jaxpr/reduce_sum | solution.py:54
  299.7 0.5 copy.87
  300.2 7.2 %bitcast_add_fusion.3 = f32[256,8,2,128]{0,3,2,1:T(8,128)} fusion(f32[256,8,2,128]{0,3,2,1:T(8,128)} %get-tuple-element.294, bf16[512,8,128,1]{0,2,3,1:T(8,128)(2,1)S(1)} %bitcast.115, f32[8,512,256,2]{2,1,3,0:T(8,128)} %get-tuple-element.274, f32[256,8,2]{0,2,1:T(2,128)S(1)} %fusion.73, pred[256,512]{0,1:T(8,128)(4,1)S(1)} %compare_and_fusion.2, ...), kind=kOutput, calls=%fused_computation.10.clone.1 | convolution fusion | flops 548929536 | bytes 13795329 | tf_op jit(solution)/shard_map/while/body/eval_jaxpr/tkgs,skd->tkgd/dot_general | solution.py:55
  307.7 1.7 constant_dynamic-slice_fusion.8
  310.0 6.0 %fusion.72 = (f32[256,8,2]{0,2,1:T(2,128)S(1)}, f32[8,512,256,2]{2,1,3,0:T(8,128)}) fusion(pred[256,512]{0,1:T(8,128)(4,1)S(1)} %compare_and_fusion.2, bf16[512,8,128,1]{0,2,3,1:T(8,128)(2,1)S(1)} %bitcast.114, bf16[256,8,2,128]{3,0,2,1:T(8,128)(2,1)} %get-tuple-element.313), kind=kOutput, calls=%fused_computation.5.clone.1 | convolution fusion | flops 543158272 | bytes 10633216 | tf_op jit(solution)/shard_map/while/body/eval_jaxpr/tkgd,skd->tkgs/dot_general | solution.py:44
  316.0 4.5 %fusion.74 = f32[256,8,2]{0,2,1:T(2,128)S(1)} fusion(f32[8,512,256,2]{2,1,3,0:T(8,128)} %get-tuple-element.274, f32[256,8,2]{0,2,1:T(2,128)S(1)} %fusion.73, pred[256,512]{0,1:T(8,128)(4,1)S(1)} %compare_and_fusion.2), kind=kLoop, calls=%fused_computation.7.clone.1 | loop fusion | flops 10481664 | bytes 8552448 | tf_op jit(solution)/shard_map/while/body/eval_jaxpr/reduce_sum | solution.py:54
  321.1 7.8 %bitcast_add_fusion.3 = f32[256,8,2,128]{0,3,2,1:T(8,128)} fusion(f32[256,8,2,128]{0,3,2,1:T(8,128)} %get-tuple-element.294, bf16[512,8,128,1]{0,2,3,1:T(8,128)(2,1)S(1)} %bitcast.115, f32[8,512,256,2]{2,1,3,0:T(8,128)} %get-tuple-element.274, f32[256,8,2]{0,2,1:T(2,128)S(1)} %fusion.73, pred[256,512]{0,1:T(8,128)(4,1)S(1)} %compare_and_fusion.2, ...), kind=kOutput, calls=%fused_computation.10.clone.1 | convolution fusion | flops 548929536 | bytes 13795329 | tf_op jit(solution)/shard_map/while/body/eval_jaxpr/tkgs,skd->tkgd/dot_general | solution.py:55
  329.1 1.7 constant_dynamic-slice_fusion.8
  331.4 6.0 %fusion.72 = (f32[256,8,2]{0,2,1:T(2,128)S(1)}, f32[8,512,256,2]{2,1,3,0:T(8,128)}) fusion(pred[256,512]{0,1:T(8,128)(4,1)S(1)} %compare_and_fusion.2, bf16[512,8,128,1]{0,2,3,1:T(8,128)(2,1)S(1)} %bitcast.114, bf16[256,8,2,128]{3,0,2,1:T(8,128)(2,1)} %get-tuple-element.313), kind=kOutput, calls=%fused_computation.5.clone.1 | convolution fusion | flops 543158272 | bytes 10633216 | tf_op jit(solution)/shard_map/while/body/eval_jaxpr/tkgd,skd->tkgs/dot_general | solution.py:44
  337.5 4.5 %fusion.74 = f32[256,8,2]{0,2,1:T(2,128)S(1)} fusion(f32[8,512,256,2]{2,1,3,0:T(8,128)} %get-tuple-element.274, f32[256,8,2]{0,2,1:T(2,128)S(1)} %fusion.73, pred[256,512]{0,1:T(8,128)(4,1)S(1)} %compare_and_fusion.2), kind=kLoop, calls=%fused_computation.7.clone.1 | loop fusion | flops 10481664 | bytes 8552448 | tf_op jit(solution)/shard_map/while/body/eval_jaxpr/reduce_sum | solution.py:54
  342.5 7.8 %bitcast_add_fusion.3 = f32[256,8,2,128]{0,3,2,1:T(8,128)} fusion(f32[256,8,2,128]{0,3,2,1:T(8,128)} %get-tuple-element.294, bf16[512,8,128,1]{0,2,3,1:T(8,128)(2,1)S(1)} %bitcast.115, f32[8,512,256,2]{2,1,3,0:T(8,128)} %get-tuple-element.274, f32[256,8,2]{0,2,1:T(2,128)S(1)} %fusion.73, pred[256,512]{0,1:T(8,128)(4,1)S(1)} %compare_and_fusion.2, ...), kind=kOutput, calls=%fused_computation.10.clone.1 | convolution fusion | flops 548929536 | bytes 13795329 | tf_op jit(solution)/shard_map/while/body/eval_jaxpr/tkgs,skd->tkgd/dot_general | solution.py:55
  350.6 1.7 constant_dynamic-slice_fusion.8
  352.9 6.0 %fusion.72 = (f32[256,8,2]{0,2,1:T(2,128)S(1)}, f32[8,512,256,2]{2,1,3,0:T(8,128)}) fusion(pred[256,512]{0,1:T(8,128)(4,1)S(1)} %compare_and_fusion.2, bf16[512,8,128,1]{0,2,3,1:T(8,128)(2,1)S(1)} %bitcast.114, bf16[256,8,2,128]{3,0,2,1:T(8,128)(2,1)} %get-tuple-element.313), kind=kOutput, calls=%fused_computation.5.clone.1 | convolution fusion | flops 543158272 | bytes 10633216 | tf_op jit(solution)/shard_map/while/body/eval_jaxpr/tkgd,skd->tkgs/dot_general | solution.py:44
  358.9 4.5 %fusion.74 = f32[256,8,2]{0,2,1:T(2,128)S(1)} fusion(f32[8,512,256,2]{2,1,3,0:T(8,128)} %get-tuple-element.274, f32[256,8,2]{0,2,1:T(2,128)S(1)} %fusion.73, pred[256,512]{0,1:T(8,128)(4,1)S(1)} %compare_and_fusion.2), kind=kLoop, calls=%fused_computation.7.clone.1 | loop fusion | flops 10481664 | bytes 8552448 | tf_op jit(solution)/shard_map/while/body/eval_jaxpr/reduce_sum | solution.py:54
  363.4 0.5 copy.87
  364.0 7.8 %bitcast_add_fusion.3 = f32[256,8,2,128]{0,3,2,1:T(8,128)} fusion(f32[256,8,2,128]{0,3,2,1:T(8,128)} %get-tuple-element.294, bf16[512,8,128,1]{0,2,3,1:T(8,128)(2,1)S(1)} %bitcast.115, f32[8,512,256,2]{2,1,3,0:T(8,128)} %get-tuple-element.274, f32[256,8,2]{0,2,1:T(2,128)S(1)} %fusion.73, pred[256,512]{0,1:T(8,128)(4,1)S(1)} %compare_and_fusion.2, ...), kind=kOutput, calls=%fused_computation.10.clone.1 | convolution fusion | flops 548929536 | bytes 13795329 | tf_op jit(solution)/shard_map/while/body/eval_jaxpr/tkgs,skd->tkgd/dot_general | solution.py:55
  371.8 1.8 divide_convert_fusion
  373.6 1.4 copy.78
  (100 shorter events, 8.2 us)
Async XLA Ops:
  7.2 42.5 %copy-start = (s32[16,8]{0,1:T(8,128)S(1)}, s32[16,8]{0,1:T(8,128)}, u32[]{:S(2)}) copy-start(s32[16,8]{0,1:T(8,128)} %param.21) | copy-start | bytes 1540
  7.2 42.7 %copy-start.6 = (s32[16,4]{0,1:T(4,128)S(1)}, s32[16,4]{0,1:T(4,128)}, u32[]{:S(2)}) copy-start(s32[16,4]{0,1:T(4,128)} %param.20) | copy-start | bytes 772
  7.2 43.3 %copy-start.3 = (bf16[1,1,256,2048]{3,2,1,0:T(8,128)(2,1)S(1)}, bf16[1,1,256,2048]{3,2,1,0:T(8,128)(2,1)}, u32[]{:S(2)}) copy-start(bf16[1,1,256,2048]{3,2,1,0:T(8,128)(2,1)} %param.13) | copy-start | bytes 3145732
  7.2 67.8 %all-gather.6.cloned.1.call-start = ((), (), s32[]{:S(2)}) async-start(), calls=%async_computation.2 | async-start | bytes 4456448 | tf_op jit(solution)/shard_map/all_gather | solution.py:166
  22.5 106.0 %all-gather.12.cloned.1.call-start = ((), (), s32[]{:S(2)}) async-start(), calls=%async_computation.5 | async-start | bytes 4456448 | tf_op jit(solution)/shard_map/all_gather | solution.py:167
  35.1 185.0 %all-gather.10.cloned.1.call-start = ((), (), s32[]{:S(2)}) async-start(), calls=%async_computation.4 | async-start | bytes 8912896 | tf_op jit(solution)/shard_map/all_gather | solution.py:165
  49.6 203.4 %all-gather.8.cloned.1.call-start = ((), (), s32[]{:S(2)}) async-start(), calls=%async_computation.3 | async-start | bytes 4718592 | tf_op jit(solution)/shard_map/all_gather | solution.py:179
  75.0 6.5 %copy-start.9 = (f32[2048]{0:T(1024)S(1)}, f32[2048]{0:T(1024)}, u32[]{:S(2)}) copy-start(f32[2048]{0:T(1024)} %param.14) | copy-start | bytes 24580
  81.5 3.6 copy-start.7
  86.6 46.1 %copy-start.5 = (s32[1,1,256]{2,1,0:T(1,128)S(1)}, s32[1,1,256]{2,1,0:T(1,128)}, u32[]{:S(2)}) copy-start(s32[1,1,256]{2,1,0:T(1,128)} %param.22) | copy-start | bytes 3076
  86.6 57.0 %copy-start.2 = (bf16[256,1024]{1,0:T(8,128)(2,1)S(1)}, bf16[256,1024]{1,0:T(8,128)(2,1)}, u32[]{:S(2)}) copy-start(bf16[256,1024]{1,0:T(8,128)(2,1)} %copy.65) | copy-start | bytes 1572868
  86.6 200.0 %all-gather.14.cloned.1.call-start = ((), (), s32[]{:S(2)}) async-start(), calls=%async_computation.6 | async-start | bytes 4718592 | tf_op jit(solution)/shard_map/all_gather | solution.py:180
  135.7 17.5 %all-to-all-start = ((s32[128,1,4]{2,1,0:T(1,128)}), s32[128,1,4]{2,1,0:T(1,128)S(1)}, u32[]{:S(2)}, u32[]{:S(2)}) async-start(s32[128,1,4]{2,1,0:T(1,128)} %bitcast.26), calls=%async_computation | async-start | bytes 131072 | tf_op jit(solution)/shard_map/all_to_all | solution.py:218
  153.2 53.2 %all-to-all-start.1 = ((bf16[128,4,2048]{2,1,0:T(4,128)(2,1)}), bf16[128,4,2048]{2,1,0:T(4,128)(2,1)S(1)}, u32[]{:S(2)}, u32[]{:S(2)}) async-start(bf16[128,4,2048]{2,1,0:T(4,128)(2,1)} %reshape.385), calls=%async_computation.1 | async-start | bytes 4194304 | tf_op jit(solution)/shard_map/all_to_all | solution.py:211
  220.1 12.5 %copy-start.4 = (bf16[1,1,256,2048]{3,2,1,0:T(8,128)(2,1)S(1)}, bf16[1,1,256,2048]{3,2,1,0:T(8,128)(2,1)}, u32[]{:S(2)}) copy-start(bf16[1,1,256,2048]{3,2,1,0:T(8,128)(2,1)} %param.13) | copy-start | bytes 3145732
  232.6 6.0 %copy-start.8 = (f32[128]{0:T(128)S(1)}, f32[128]{0:T(128)}, u32[]{:S(2)}) copy-start(f32[128]{0:T(128)} %param.18) | copy-start | bytes 1540
  371.8 3.2 copy-start.1
Sparse Core Ops, SparseCore 0:
  22.6 52.4 all-gather.5
  77.2 51.2 all-gather.11
  130.6 89.4 all-gather.9
  221.7 31.2 all-gather.7
  254.5 32.0 all-gather.13
where the time goes:
time: 383 us; the launch traced here: 382 us
  waiting for transfers between devices  167 us (44%)
  matrix products  68.6 us (18%)
  local copies, waits for them, and re-layouts  48 us (13%)
  blocking collectives  42.2 us (11%)
  other arithmetic  27.9 us (7%)
  between operations  14.1 us (4%)
  starting transfers between devices  13.8 us (4%)
    all_to_all x1, waiting for transfers between devices, shards(): lax.all_to_all(bucket.reshape(owner_count, per_owner, kv_width), ('ctx',...  45.7 us
    all_gather x1, waiting for transfers between devices, shards(): lax.all_gather(value_cols, 'fsdp', axis=0, tiled=True)  41.8 us
    all_gather x1, waiting for transfers between devices, shards(): lax.all_gather(value_new, 'ctx', axis=0, tiled=True)  33.7 us
    dot_general x4, matrix products, attend_keys(): jnp.einsum('tkgs,skd->tkgd', weights.astype(jnp.bfloat16), heads_of_value...  30.7 us
    dot_general x4, matrix products, attend_keys(): jnp.einsum('tkgd,skd->tkgs', heads_of_query, heads_of_key, preferred_elem...  24.1 us
    all_gather x1, waiting for transfers between devices, shards(): lax.all_gather(key_cols, 'fsdp', axis=0, tiled=True)  23.9 us
    dot_general x2, local copies, waits for them, and re-layouts, project_rows(): jnp.dot(source, shard_rows, preferred_element_type=jnp.float32)  19 us
    reduce_sum x4, other arithmetic, attend_keys(): row_sum = row_sum * shrink + jnp.sum(weights, axis=-1)  17.9 us
  transfers between devices with their start and end apart: 7, of which 7 were waited for; matrix products, arithmetic and copies ran while one was open for 15% of the time, Pallas kernels for 0%

commit v1 on v0

v1 whole, which is shorter than its diff:
```python
import math

import jax
import jax.numpy as jnp
from jax import lax
from jax.experimental import pallas as pl
from jax.experimental.pallas import tpu as pltpu
from jax.sharding import Mesh, PartitionSpec as P

HEAD = 128
TOK = 256
EPSILON = 1e-06
THETA = 1000000.0
NEG_BIG = -1e30
MOST = 4
MIB = 1 << 20
ROUTE = 8
CTX = ("y", "core")
FSDP = ("x", "z")


def shift(value, axis, by):
    size = lax.axis_size(axis)
    return lax.ppermute(value, axis, [(i, (i + by) % size) for i in range(size)])


def norm_rope(raw, gain, cos, sin):
    factor = lax.rsqrt(jnp.mean(raw * raw, axis=-1, keepdims=True) + EPSILON)
    normal = raw * factor * gain
    return (normal * cos + pltpu.roll(normal, HEAD // 2, 1) * sin).astype(jnp.bfloat16)


def call(kernel, out_shape, specs, outs, mib, cost, name, scratch=(), grid=(), maps=()):
    flops, moved = cost
    return pl.pallas_call(
        kernel,
        grid_spec=pltpu.PrefetchScalarGridSpec(
            num_scalar_prefetch=len(maps),
            grid=grid,
            in_specs=specs,
            out_specs=outs,
            scratch_shapes=scratch,
        ),
        out_shape=out_shape,
        compiler_params=pltpu.CompilerParams(vmem_limit_bytes=mib * MIB),
        cost_estimate=pl.CostEstimate(flops=flops, bytes_accessed=moved * MIB, transcendentals=0),
        name=name,
    )


def shape(*dims, dtype=jnp.bfloat16):
    return jax.ShapeDtypeStruct(dims, dtype)


WHOLE = pl.BlockSpec(memory_space=pltpu.VMEM)
FAR = pl.BlockSpec(memory_space=pltpu.HBM)


def pack_kernel(hidden, routes, out, sem):
    move = pltpu.make_async_copy(hidden, out.at[pl.ds(ROUTE, TOK)], sem)
    move.start()
    out[0:ROUTE, :] = jnp.zeros((ROUTE, out.shape[1]), out.dtype)
    out[0:1, 0:TOK] = routes[...].astype(out.dtype)
    move.wait()


def pack(hidden, routes):
    return call(
        pack_kernel,
        shape(ROUTE + TOK, 2048),
        [FAR, WHOLE],
        WHOLE,
        4,
        (0, 2),
        "pack",
        [pltpu.SemaphoreType.DMA],
    )(hidden, routes)


def spread_weights_kernel(a, b, c, routes, out, part, sems):
    moves = [
        pltpu.make_async_copy(a, part.at[:, pl.ds(0, 2 * HEAD)], sems.at[0]),
        pltpu.make_async_copy(b, part.at[:, pl.ds(2 * HEAD, HEAD)], sems.at[1]),
        pltpu.make_async_copy(c, part.at[:, pl.ds(3 * HEAD, HEAD)], sems.at[2]),
    ]
    for move in moves:
        move.start()
    for i in range(16):
        out[i, 0:ROUTE, 0:HEAD] = routes[i]
        out[i, 0:ROUTE, HEAD:] = jnp.zeros((ROUTE, 3 * HEAD), out.dtype)
    for move in moves:
        move.wait()
    for i in range(16):
        out[i, ROUTE:, :] = part[...]


def spread_weights(a, b, c, routes):
    return call(
        spread_weights_kernel,
        shape(16, ROUTE + 128, 4 * HEAD),
        [FAR, FAR, FAR, WHOLE],
        WHOLE,
        6,
        (0, 3),
        "spread_weights",
        [pltpu.VMEM((128, 4 * HEAD), jnp.bfloat16), pltpu.SemaphoreType.DMA((3,))],
    )(a, b, c, routes)


def join_kernel(got, w_q, w_kv, routes):
    for i in range(16):
        w_q[i * 128 : (i + 1) * 128, :] = got[i, ROUTE:, 0 : 2 * HEAD]
        w_kv[i * 128 : (i + 1) * 128, :] = got[i, ROUTE:, 2 * HEAD :]
        routes[i] = got[i, 0:ROUTE, 0:HEAD]


def join_weights(got):
    return call(
        join_kernel,
        [shape(2048, 2 * HEAD), shape(2048, 2 * HEAD), shape(16, ROUTE, HEAD)],
        [WHOLE],
        [WHOLE] * 3,
        6,
        (0, 4),
        "join_weights",
    )(got)


def owner_row(ref):
    own = ref[0:ROUTE, 0:TOK].astype(jnp.float32)
    column = jnp.transpose(own)[:, 0:1]
    row = own[0:1]
    token = lax.broadcasted_iota(jnp.int32, (TOK, TOK), 0)
    other = lax.broadcasted_iota(jnp.int32, (TOK, TOK), 1)
    same = (column == row) & (token < other)
    rank = jnp.sum(same.astype(jnp.float32), axis=0, keepdims=True)
    return (row * 8 + rank).astype(jnp.int32)


def normalize(pairs, core, gain):
    count = sum(len(p) for p in pairs)

    def kernel(core_ref, *refs):
        gain_ref, out, codes = refs[count:]
        at = 0
        for i, p in enumerate(pairs):
            row, side = 0, 0
            for source in refs[at : at + len(p)]:
                start = source.shape[0] % 16
                if start:
                    mine = core_ref[0] + side - 2 * core_ref[0] * side
                    codes[i, :, side * TOK : (side + 1) * TOK] = owner_row(source) + mine * MOST
                    side += 1
                for j in range(start, source.shape[0], 128):
                    x = source[j : j + 128, :].astype(jnp.float32)
                    factor = lax.rsqrt(jnp.mean(x * x, axis=-1, keepdims=True) + EPSILON)
                    out[i, row : row + 128, :] = (x * factor * gain_ref[...]).astype(jnp.bfloat16)
                    row += 128
            at += len(p)

    n = len(pairs)
    return call(
        kernel,
        [shape(n, 2 * TOK, 2048), shape(n, 1, 2 * TOK, dtype=jnp.int32)],
        [pl.BlockSpec(memory_space=pltpu.SMEM)] + [WHOLE] * (count + 1),
        [WHOLE] * 2,
        18,
        (8 * n * MIB, 4 * n),
        "normalize",
    )(core, *(x for p in pairs for x in p), gain)


def keys_kernel(
    ys, piece_of, x_a, x_b, code_a, code_b, w, gain, cos, sin, k_out, v_out, b_out, kv
):
    pair = pl.program_id(0)

    def go(x, code):
        raw = jnp.dot(x, w[...], preferred_element_type=jnp.float32)
        key = norm_rope(raw[:, :HEAD], gain[...], cos[0], sin[0])
        value = raw[:, HEAD:].astype(jnp.bfloat16)
        for side in range(2):
            at = pl.multiple_of(piece_of[2 * pair + side] * TOK, TOK)
            k_out[pl.ds(at, TOK), :] = key[side * TOK : (side + 1) * TOK]
            v_out[pl.ds(at, TOK), :] = value[side * TOK : (side + 1) * TOK]
        kv[:, :HEAD] = key
        kv[:, HEAD:] = value
        place = lax.broadcasted_iota(jnp.int32, (8 * 128, 2 * TOK), 0)
        pick = (place == code).astype(jnp.bfloat16)
        got = jnp.dot(pick, kv[...], preferred_element_type=jnp.float32)
        b_out[...] = got.reshape(128, 8, 2 * HEAD).astype(jnp.bfloat16)

    pl.when(pair < 3)(lambda: go(x_a[jnp.minimum(pair, 2)], code_a[jnp.minimum(pair, 2)]))
    pl.when(pair == 3)(lambda: go(x_b[0], code_b[0]))


def keys(y_of_pair, piece_of, x_a, x_b, code_a, code_b, w, gain, cos, sin):
    maps = y_of_pair, piece_of
    table = pl.BlockSpec((1, 2 * TOK, HEAD), lambda i, *_: (i, 0, 0))
    stream = pl.BlockSpec((8 * TOK, HEAD), lambda i, *_: (0, 0))
    return call(
        keys_kernel,
        [shape(8 * TOK, HEAD), shape(8 * TOK, HEAD), shape(128, 32, 2 * HEAD)],
        [WHOLE] * 6 + [table] * 2,
        [stream, stream, pl.BlockSpec((128, 8, 2 * HEAD), lambda i, ys, _: (0, ys[i], 0))],
        12,
        (2 * 2048 * 2048 * 256, 12),
        "keys",
        [pltpu.VMEM((2 * TOK, 2 * HEAD), jnp.bfloat16)],
        (4,),
        maps,
    )(*maps, x_a, x_b, code_a, code_b, w, gain, cos, sin)


def queries_kernel(x_a, x_b, w, gain, cos, sin, out):
    pair = pl.program_id(0)

    def go(x):
        raw = jnp.dot(x, w[...], preferred_element_type=jnp.float32)
        for h in range(2):
            part = slice(h * HEAD, (h + 1) * HEAD)
            out[0, :, part] = norm_rope(raw[:, part], gain[...], cos[0], sin[0])

    pl.when(pair < 3)(lambda: go(x_a[jnp.minimum(pair, 2)]))
    pl.when(pair == 3)(lambda: go(x_b[0]))


def queries(x_a, x_b, w, gain, cos, sin):
    table = pl.BlockSpec((1, 2 * TOK, HEAD), lambda i: (i, 0, 0))
    return call(
        queries_kernel,
        shape(4, 2 * TOK, 2 * HEAD),
        [WHOLE] * 4 + [table] * 2,
        pl.BlockSpec((1, 2 * TOK, 2 * HEAD), lambda i: (i, 0, 0)),
        12,
        (2 * 2048 * 2048 * 256, 12),
        "queries",
        (),
        (4,),
    )(x_a, x_b, w, gain, cos, sin)


def attend_kernel(piece_of, ctx_of, low, starts, q, keys, values, lead, out):
    p = piece_of[pl.program_id(0)]
    lo = low[p]
    out[0, 0:ROUTE, :] = lead[0]
    both = jnp.concatenate([q[0, :, :HEAD], q[0, :, HEAD:]], axis=0)
    place = p * TOK + jnp.bitwise_and(lax.broadcasted_iota(jnp.int32, (2 * TOK, 1), 0), TOK - 1)
    begin = jnp.zeros_like(place)
    for n in range(1, 4):
        begin = jnp.where(starts[n] <= place, starts[n], begin)

    def blocks(count):
        at = pl.multiple_of(lo * TOK, TOK)
        span = count * TOK
        s = lax.dot_general(
            both,
            keys[pl.ds(at, span), :],
            (((1,), (1,)), ((), ())),
            preferred_element_type=jnp.float32,
        )
        spot = at + lax.broadcasted_iota(jnp.int32, (1, span), 1)
        s = jnp.where((spot <= place) & (spot >= begin), s, NEG_BIG)
        top = jnp.max(s, axis=1, keepdims=True)
        e = jnp.exp((s - top) * (1.0 / math.sqrt(HEAD)))
        total = jnp.sum(e, axis=1, keepdims=True)
        mixed = jnp.dot(
            e.astype(jnp.bfloat16), values[pl.ds(at, span), :], preferred_element_type=jnp.float32
        )
        mixed = (mixed / total).astype(jnp.bfloat16)
        out[0, ROUTE:, :HEAD] = mixed[:TOK]
        out[0, ROUTE:, HEAD:] = mixed[TOK:]

    for count in range(1, 6):
        pl.when(p + 1 - lo == count)(lambda count=count: blocks(count))


def attend(piece_of, ctx_of, low, starts, q, k, v, leads):
    maps = piece_of, ctx_of, low, starts
    return call(
        attend_kernel,
        shape(8, ROUTE + TOK, 2 * HEAD),
        [
            pl.BlockSpec((1, TOK, 2 * HEAD), lambda i, *_: (i, 0, 0)),
            WHOLE,
            WHOLE,
            pl.BlockSpec((1, ROUTE, 2 * HEAD), lambda i, p, c, *_: (c[i], 0, 0)),
        ],
        pl.BlockSpec((1, ROUTE + TOK, 2 * HEAD), lambda i, *_: (i, 0, 0)),
        14,
        (8 * 2048 * 2048 * 128, 4),
        "attend",
        (),
        (8,),
        maps,
    )(*maps, q.reshape(8, TOK, 2 * HEAD), k, v, leads)


def cache_kernel(slots, got, out):
    rows = lax.broadcasted_iota(jnp.int32, (512, 512), 0)
    pick = (rows == slots[...]).astype(jnp.bfloat16)
    for c in range(8):
        put = jnp.dot(pick, got[c], preferred_element_type=jnp.float32).astype(jnp.bfloat16)
        out[:, c * HEAD : (c + 1) * HEAD] = put[:, :HEAD]
        out[:, (8 + c) * HEAD : (9 + c) * HEAD] = put[:, HEAD:]


def fill_cache(slots, got):
    whole = pl.BlockSpec(memory_space=pltpu.VMEM)
    return pl.pallas_call(
        cache_kernel,
        out_shape=jax.ShapeDtypeStruct((512, 2048), jnp.bfloat16),
        in_specs=[whole, whole],
        out_specs=whole,
        compiler_params=pltpu.CompilerParams(vmem_limit_bytes=32 * MIB),
        cost_estimate=pl.CostEstimate(
            flops=2 * 512 * 512 * 2048, bytes_accessed=4 * MIB, transcendentals=0
        ),
        name="fill_cache",
    )(slots, got)


def spread_kernel(ctx_of, *refs):
    out, leads = refs[-2:]
    side = 0
    for ref in refs[:-2]:
        for i in range(ref.shape[0]):
            ctx = ctx_of[side]
            out[:, pl.ds(pl.multiple_of(ctx * 2 * HEAD, 2 * HEAD), 2 * HEAD)] = ref[i, ROUTE:]
            leads[ctx] = ref[i, 0:ROUTE, 0:HEAD].astype(jnp.float32)
            side += 1


def spread(ctx_of, parts):
    return call(
        spread_kernel,
        [shape(TOK, 2048), shape(8, ROUTE, HEAD, dtype=jnp.float32)],
        [pl.BlockSpec(memory_space=pltpu.SMEM)] + [WHOLE] * len(parts),
        [WHOLE] * 2,
        6,
        (0, 2),
        "spread",
    )(ctx_of, *parts)


def choose(index, table):
    hit = index[:, None] == jnp.arange(table.shape[0], dtype=jnp.int32)[None, :]
    return jnp.sum(jnp.where(hit, table[None], 0), axis=1, dtype=jnp.int32)


def ring(value, axis, half):
    below, above = shift(value, axis, 1), shift(value, axis, -1)
    return [value, above, below, shift(above[:half], axis, -1), shift(below[half:], axis, 1)]


def shards(
    hidden, norm_gain, w_query, w_key, w_value, q_gain, k_gain, lengths, piece_map, owner, slot
):
    y, core = lax.axis_index("y"), lax.axis_index("core")
    group = lax.axis_index(FSDP)
    own = owner[0, 0]
    offsets = jnp.array([0, 1, 3, 2], jnp.int32)

    h = pack(hidden[0, 0], own[None])
    near, above, below, far_lo, far_hi = ring(h, "y", ROUTE + TOK // 2)
    swap = lambda value: shift(value, "core", 1)
    pairs = [
        (near, swap(near)),
        (above, swap(above)),
        (below, swap(below)),
        (far_lo, far_hi, swap(far_lo), swap(far_hi)),
    ]

    token = jnp.arange(TOK, dtype=jnp.int32)
    same = (own[:, None] == own[None, :]) & (token[None, :] < token[:, None])
    rank = jnp.sum(same.astype(jnp.int32), axis=1, dtype=jnp.int32)
    spot = (own % 16) * 32 + (own // 16) * MOST + rank
    hit = spot[None, :] == jnp.arange(512, dtype=jnp.int32)[:, None]
    table = jnp.sum(jnp.where(hit, slot[0, 0][None, :] + 1, 0), axis=1, dtype=jnp.int32)
    table = table.reshape(16, 1, 32)
    table = jnp.concatenate([table // 16, table % 16], axis=1).astype(jnp.bfloat16)
    table = jnp.pad(table, ((0, 0), (0, ROUTE - 2), (0, HEAD - 32)))
    _, table = lax.optimization_barrier((h, table))
    w = spread_weights(w_query, w_key, w_value, table)
    w = lax.all_to_all(w, FSDP, split_axis=0, concat_axis=0, tiled=True)
    w_q, w_kv, leads = join_weights(w)
    leads = leads[:, :2, :32].reshape(16, 2, 8, MOST).transpose(2, 1, 0, 3).reshape(8, 2, 64)
    leads = jnp.pad(leads, ((0, 0), (0, ROUTE - 2), (0, 2 * HEAD - 64)))

    my_pieces = lax.dynamic_index_in_dim(piece_map, group, 0, keepdims=False)
    my_lengths = lax.dynamic_index_in_dim(lengths, group, 0, keepdims=False)
    ends = jnp.cumsum(my_lengths, dtype=jnp.int32)
    starts = ends - my_lengths
    y_of_pair = ((y + offsets) % 4).astype(jnp.int32)
    core_of = jnp.stack([core, 1 - core]).astype(jnp.int32)
    ctx_of_slot = (y_of_pair[:, None] * 2 + core_of[None, :]).reshape(-1)
    piece_of_slot = choose(ctx_of_slot, my_pieces)
    eight = jnp.arange(8, dtype=jnp.int32)

    def begin_of(places):
        reached = starts[None, :] <= places.reshape(-1, 1)
        return jnp.max(jnp.where(reached, starts[None, :], 0), axis=1).reshape(places.shape)

    low = begin_of(eight * TOK) // TOK
    places = piece_of_slot[:, None] * TOK + jnp.arange(TOK, dtype=jnp.int32)[None, :]
    relative = places - begin_of(places)
    half = HEAD // 2
    frequency = jnp.exp(jnp.arange(half, dtype=jnp.float32) * (-2.0 * math.log(THETA) / HEAD))
    angles = relative.astype(jnp.float32).reshape(4, 2 * TOK, 1) * frequency
    cos, sin = jnp.cos(angles), jnp.sin(angles)
    cos = jnp.concatenate([cos, cos], axis=-1)
    sin = jnp.concatenate([-sin, sin], axis=-1)

    core = core.astype(jnp.int32)[None]
    x_a, code_a = normalize(pairs[:3], core, norm_gain[None])
    x_b, code_b = normalize(pairs[3:], core, norm_gain[None])
    k, v, buckets = keys(
        y_of_pair, piece_of_slot, x_a, x_b, code_a, code_b, w_kv, k_gain[None], cos, sin
    )
    buckets, x_a = lax.optimization_barrier((buckets, x_a))
    got = lax.all_to_all(buckets, CTX + FSDP, split_axis=0, concat_axis=0, tiled=True)
    q = queries(x_a, x_b, w_q, q_gain[None], cos, sin)
    mixed = attend(piece_of_slot, ctx_of_slot, low, starts, q, k, v, leads)
    mixed = mixed.reshape(4, 2, ROUTE + TOK, 2 * HEAD)
    from_above = shift(mixed[2:], "y", -1)
    from_below = shift(mixed[1], "y", 1)
    from_far = shift(from_above[1], "y", -1)
    mine = [mixed[0], from_above[0], from_below, from_far]
    other = [swap(m[1]) for m in mine]
    parts = [p for m, o in zip(mine, other) for p in (m[0][None], o[None])]
    attended, leads = spread(ctx_of_slot, parts)
    table = (leads[:, 0] * 16 + leads[:, 1]).astype(jnp.int32)[:, :64] - 1
    table = table.reshape(8, 16, MOST).transpose(1, 0, 2).reshape(1, 512)
    cache = fill_cache(table, got.reshape(8, 512, 2 * HEAD))
    return attended[None, None], cache


def solution(mesh):
    split = Mesh(mesh.devices.reshape(4, 2, 4, 4), (*CTX, *FSDP))
    placed = (
        P(CTX, FSDP, None, None),
        P(),
        P(FSDP, CTX),
        P(FSDP, CTX),
        P(FSDP, CTX),
        P(),
        P(),
        P(),
        P(),
        P(CTX, FSDP, None),
        P(CTX, FSDP, None),
    )
    return jax.shard_map(
        shards,
        mesh=split,
        in_specs=placed,
        out_specs=(P(CTX, FSDP, None, None), P((*CTX, *FSDP), None)),
        check_vma=False,
    )
```

time: 383 us -> 138 us (0.36)
  waiting for transfers between devices: 167 us -> 29.4 us
  matrix products: 68.6 us -> 0 us
  blocking collectives: 42.2 us -> 0 us
  Pallas kernels: 0 us -> 41.8 us
  local copies, waits for them, and re-layouts: 48 us -> 17.6 us
  starting transfers between devices: 13.8 us -> 41.7 us
  other arithmetic: 27.9 us -> 5.63 us
  between operations: 14.1 us -> 1.17 us
    all_gather x5 -> x0, waiting for transfers between devices: 117 us -> none  [the longest x1 41.8 us: shards(): lax.all_gather(value_cols, 'fsdp', axis=0, tiled=True)]
    dot_general x11 -> x0, matrix products: 68.6 us -> none  [the longest x4 30.7 us: attend_keys(): jnp.einsum('tkgs,skd->tkgd', weights.astype(jnp.bfloat16), heads_of_value...]
    all_to_all x2, waiting for transfers between devices: 49.8 us -> 0.29 us  [the longest x1 0.28 us: shards(): w = lax.all_to_all(w, FSDP, split_axis=0, concat_axis=0, tiled=True)]
    all_gather x3 -> x0, blocking collectives: 42.2 us -> none  [the longest x1 15.2 us: shards(): lax.all_gather(w_key, 'ctx', axis=1, tiled=True)]
    pallas_call x0 -> x10, Pallas kernels: none -> 41.8 us  [the longest x1 10.9 us: attend(): call(attend_kernel, shape(8, ROUTE + TOK, 2 * HEAD), [pl.BlockSpec((1, TO...]
    ppermute x0 -> x16, waiting for transfers between devices: none -> 29.1 us  [shift(): lax.ppermute(value, axis, [(i, (i + by) % size) for i in range(size)])]
    ppermute x0 -> x16, starting transfers between devices: none -> 23.1 us  [shift(): lax.ppermute(value, axis, [(i, (i + by) % size) for i in range(size)])]
    dot_general x2 -> x0, local copies, waits for them, and re-layouts: 19 us -> none  [project_rows(): jnp.dot(source, shard_rows, preferred_element_type=jnp.float32)]
  transfers between devices with their start and end apart: 7 -> 18, of which waited for: 7 -> 6; matrix products, arithmetic and copies ran while one was open for 15% -> 7% of each run, Pallas kernels for 0% -> 20%
where the time goes in v1:
time: 138 us; the launch traced here: 137 us
  Pallas kernels  41.8 us (30%)
  starting transfers between devices  41.7 us (30%)
  waiting for transfers between devices  29.4 us (21%)
  local copies, waits for them, and re-layouts  17.6 us (13%)
  other arithmetic  5.63 us (4%)
    ppermute x16, waiting for transfers between devices, shift(): lax.ppermute(value, axis, [(i, (i + by) % size) for i in range(size)])  29.1 us
    ppermute x16, starting transfers between devices, shift(): lax.ppermute(value, axis, [(i, (i + by) % size) for i in range(size)])  23.1 us
    unnamed x58, local copies, waits for them, and re-layouts  14.1 us
    pallas_call x1, Pallas kernels, attend(): call(attend_kernel, shape(8, ROUTE + TOK, 2 * HEAD), [pl.BlockSpec((1, TO...  10.9 us
    all_to_all x1, starting transfers between devices, shards(): lax.all_to_all(buckets, CTX + FSDP, split_axis=0, concat_axis=0, tiled=True)  10.8 us
    pallas_call x1, Pallas kernels, keys(): call(keys_kernel, [shape(8 * TOK, HEAD), shape(8 * TOK, HEAD), shape(128,...  7.91 us
    pallas_call x2, Pallas kernels, normalize(): call(kernel, [shape(n, 2 * TOK, 2048), shape(n, 1, 2 * TOK, dtype=jnp.int...  7.76 us
    all_to_all x1, starting transfers between devices, shards(): w = lax.all_to_all(w, FSDP, split_axis=0, concat_axis=0, tiled=True)  7.74 us
  transfers between devices with their start and end apart: 18, of which 6 were waited for; matrix products, arithmetic and copies ran while one was open for 7% of the time, Pallas kernels for 20%

profile of v1, /device:TPU:1, one launch (start us, length us, event | category | flops | bytes accessed | tf_op | source)
XLA Modules:
  0.0 137.3 jit_solution(17146501171047954540)
XLA Ops:
  0.7 1.2 copy-done.8
  1.9 0.7 copy-done.15
  2.7 2.2 %collective-permute-start.3 = (bf16[264,2048]{1,0:T(8,128)(2,1)S(1)}, bf16[264,2048]{1,0:T(8,128)(2,1)}, u32[]{:S(2)}, u32[]{:S(2)}) collective-permute-start(bf16[264,2048]{1,0:T(8,128)(2,1)S(1)} %pack.1.refs_0_), channel_id=1, source_target_pairs={{0,32},{32,64},{64,96},{96,0},{1,33},{33,65},{65,97},{97,1},{2,34}... | collective-permute-start | bytes 3244040 | tf_op jit(solution)/shard_map/ppermute | solution.py:24
  4.9 1.5 %collective-permute-start.1 = (bf16[264,2048]{1,0:T(8,128)(2,1)S(1)}, bf16[264,2048]{1,0:T(8,128)(2,1)}, u32[]{:S(2)}, u32[]{:S(2)}) collective-permute-start(bf16[264,2048]{1,0:T(8,128)(2,1)S(1)} %pack.1.refs_0_), channel_id=1, source_target_pairs={{0,96},{32,0},{64,32},{96,64},{1,97},{33,1},{65,33},{97,65},{2,98}... | collective-permute-start | bytes 3244040 | tf_op jit(solution)/shard_map/ppermute | solution.py:24
  6.4 1.0 collective-permute-start
  7.4 0.2 convert_reduce_fusion
  8.0 1.6 %spread_weights.1 = bf16[16,136,512]{2,1,0:T(8,128)(2,1)} custom-call(bf16[128,256]{1,0:T(8,128)(2,1)S(1)} %copy-done.11, bf16[128,128]{1,0:T(8,128)(2,1)S(1)} %copy-done.12, bf16[128,128]{1,0:T(8,128)(2,1)S(1)} %copy-done.13, bf16[16,8,128]{2,1,0:T(8,128)(2,1)S(1)} %fusion.7.routes), custom_call_target="tpu_custom_call" | custom-call | bytes 3145728 | tf_op jit(solution)/shard_map/spread_weights/pallas_call | solution.py:98
  9.7 7.7 %all-to-all-start = ((bf16[16,136,512]{2,1,0:T(8,128)(2,1)}), bf16[16,136,512]{2,1,0:T(8,128)(2,1)}, u32[]{:S(2)}, u32[]{:S(2)}) async-start(bf16[16,136,512]{2,1,0:T(8,128)(2,1)} %spread_weights.1), calls=%async_computation | async-start | bytes 4456448 | tf_op jit(solution)/shard_map/all_to_all | solution.py:385
  17.7 0.2 dynamic-slice_reduce_fusion
  17.9 0.2 select_reduce_fusion.2.piece_of
  18.4 0.2 reduce-window.4
  18.8 11.1 %collective-permute-done.3.refs_4_ = bf16[264,2048]{1,0:T(8,128)(2,1)} collective-permute-done((bf16[264,2048]{1,0:T(8,128)(2,1)S(1)}, bf16[264,2048]{1,0:T(8,128)(2,1)}, u32[]{:S(2)}, u32[]{:S(2)}) %collective-permute-start.3) | collective-permute-done | bytes 1081376 | tf_op jit(solution)/shard_map/ppermute | solution.py:24
  29.9 1.1 slice.87
  31.0 1.1 slice.86
  32.1 2.7 %collective-permute-start.5 = (bf16[136,2048]{1,0:T(8,128)(2,1)S(1)}, bf16[136,2048]{1,0:T(8,128)(2,1)}, u32[]{:S(2)}, u32[]{:S(2)}) collective-permute-start(bf16[136,2048]{1,0:T(8,128)(2,1)S(1)} %slice.86), channel_id=1, source_target_pairs={{0,96},{32,0},{64,32},{96,64},{1,97},{33,1},{65,33},{97,65},{2,98}... | collective-permute-start | bytes 1671176 | tf_op jit(solution)/shard_map/ppermute | solution.py:24
  34.9 1.9 %collective-permute-start.4 = (bf16[264,2048]{1,0:T(8,128)(2,1)}, bf16[264,2048]{1,0:T(8,128)(2,1)}, u32[]{:S(2)}, u32[]{:S(2)}) collective-permute-start(bf16[264,2048]{1,0:T(8,128)(2,1)} %collective-permute-done.3.refs_4_), channel_id=1, source_target_pairs={{0,16},{16,0},{1,17},{17,1},{2,18},{18,2},{3,19},{19,3},{4,20},{20... | collective-permute-start | bytes 3244040 | tf_op jit(solution)/shard_map/ppermute | solution.py:24
  36.8 3.7 %fusion = (f32[4,512,64]{2,1,0:T(8,128)S(1)}, f32[4,512,64]{2,1,0:T(8,128)S(1)}, f32[4,512,64]{2,1,0:T(8,128)S(1)}) fusion(f32[64]{0:T(128)S(1)} %multiply_exponential_fusion, f32[4,512]{1,0:T(4,128)S(1)} %subtract_convert_fusion), kind=kLoop, calls=%fused_computation.6 | loop fusion | flops 262144 | bytes 1581312 | tf_op jit(solution)/shard_map/neg | solution.py:412
  40.5 0.6 pad_maximum_fusion
  41.2 3.2 %collective-permute-done.6.refs_1_ = bf16[128,2048]{1,0:T(8,128)(2,1)} collective-permute-done((bf16[128,2048]{1,0:T(8,128)(2,1)S(1)}, bf16[128,2048]{1,0:T(8,128)(2,1)}, u32[]{:S(2)}, u32[]{:S(2)}) %collective-permute-start.6) | collective-permute-done | bytes 524320 | tf_op jit(solution)/shard_map/ppermute | solution.py:24
  44.4 2.3 %collective-permute-start.8 = (bf16[128,2048]{1,0:T(8,128)(2,1)}, bf16[128,2048]{1,0:T(8,128)(2,1)}, u32[]{:S(2)}, u32[]{:S(2)}) collective-permute-start(bf16[128,2048]{1,0:T(8,128)(2,1)} %collective-permute-done.6.refs_1_), channel_id=1, source_target_pairs={{0,16},{16,0},{1,17},{17,1},{2,18},{18,2},{3,19},{19,3},{4,20},{20... | collective-permute-start | bytes 1572872 | tf_op jit(solution)/shard_map/ppermute | solution.py:24
  46.7 1.0 collective-permute-start.7
  47.8 0.3 all-to-all-done.got
  48.1 1.8 %join_weights.1 = (bf16[2048,256]{1,0:T(8,128)(2,1)S(1)}, bf16[2048,256]{1,0:T(8,128)(2,1)S(1)}, bf16[16,8,128]{2,1,0:T(8,128)(2,1)S(1)}) custom-call(bf16[16,136,512]{2,1,0:T(8,128)(2,1)} %all-to-all-done.got), custom_call_target="tpu_custom_call" | custom-call | bytes 4194304 | tf_op jit(solution)/shard_map/join_weights/pallas_call | solution.py:118
  49.9 1.0 copy-done.6
  50.9 1.0 copy-done.9
  52.2 5.2 %normalize.2 = (bf16[3,512,2048]{2,1,0:T(8,128)(2,1)S(1)}, s32[3,1,512]{2,1,0:T(1,128)S(1)}) custom-call(s32[1]{0:T(128)} %bitcast.core_ref, bf16[264,2048]{1,0:T(8,128)(2,1)S(1)} %pack.1.refs_0_, bf16[264,2048]{1,0:T(8,128)(2,1)} %collective-permute-done.refs_1_, bf16[264,2048]{1,0:T(8,128)(2,1)} %collective-permute-done.1.refs_2_, ...), custom_call_target="tpu_custom_call" | custom-call | flops 25165824 | bytes 12582912 | tf_op jit(solution)/shard_map/normalize/pallas_call | solution.py:162
  57.5 2.5 %normalize.3 = (bf16[1,512,2048]{2,1,0:T(8,128)(2,1)S(1)}, s32[1,1,512]{2,1,0:T(1,128)S(1)}) custom-call(s32[1]{0:T(128)} %bitcast.core_ref, bf16[136,2048]{1,0:T(8,128)(2,1)} %collective-permute-done.5.refs_0_, bf16[128,2048]{1,0:T(8,128)(2,1)} %collective-permute-done.6.refs_1_, bf16[136,2048]{1,0:T(8,128)(2,1)} %collective-permute-done.7.refs_2_, ...), custom_call_target="tpu_custom_call" | custom-call | flops 8388608 | bytes 4194304 | tf_op jit(solution)/shard_map/normalize/pallas_call | solution.py:162
  60.0 7.9 %keys.1 = (bf16[2048,128]{1,0:T(8,128)(2,1)S(1)}, bf16[2048,128]{1,0:T(8,128)(2,1)S(1)}, bf16[128,32,256]{2,1,0:T(8,128)(2,1)S(1)}) custom-call(s32[4]{0:T(128)S(1)} %get-tuple-element.35.ys, s32[8]{0:T(128)S(1)} %select_reduce_fusion.2.piece_of, bf16[3,512,2048]{2,1,0:T(8,128)(2,1)S(1)} %get-tuple-element.24.x_a, ...), custom_call_target="tpu_custom_call" | custom-call | flops 2147483648 | bytes 12582912 | tf_op jit(solution)/shard_map/keys/pallas_call | solution.py:201
  68.0 2.6 %copy-done.1 = bf16[3,512,2048]{2,1,0:T(8,128)(2,1)} copy-done((bf16[3,512,2048]{2,1,0:T(8,128)(2,1)}, bf16[3,512,2048]{2,1,0:T(8,128)(2,1)S(1)}, u32[]{:S(2)}) %copy-start.1) | copy-done | bytes 6291480
  70.6 1.4 %copy-done.5 = bf16[128,32,256]{2,1,0:T(8,128)(2,1)} copy-done((bf16[128,32,256]{2,1,0:T(8,128)(2,1)}, bf16[128,32,256]{2,1,0:T(8,128)(2,1)S(1)}, u32[]{:S(2)}) %copy-start.5) | copy-done | bytes 2097176
  72.0 0.8 copy-done.19
  72.8 0.8 copy-done.21
  73.6 10.8 %all-to-all-start.1 = ((bf16[128,32,256]{2,1,0:T(8,128)(2,1)}), bf16[128,32,256]{2,1,0:T(8,128)(2,1)}, u32[]{:S(2)}, u32[]{:S(2)}) async-start(bf16[128,32,256]{2,1,0:T(8,128)(2,1)} %copy-done.5), calls=%async_computation.1 | async-start | bytes 4194304 | tf_op jit(solution)/shard_map/all_to_all | solution.py:421
  84.4 2.8 %copy-done.2 = bf16[3,512,2048]{2,1,0:T(8,128)(2,1)S(1)} copy-done((bf16[3,512,2048]{2,1,0:T(8,128)(2,1)S(1)}, bf16[3,512,2048]{2,1,0:T(8,128)(2,1)}, u32[]{:S(2)}) %copy-start.2) | copy-done | bytes 6291480
  87.2 1.6 %copy-done.4 = bf16[1,512,2048]{2,1,0:T(8,128)(2,1)S(1)} copy-done((bf16[1,512,2048]{2,1,0:T(8,128)(2,1)S(1)}, bf16[1,512,2048]{2,1,0:T(8,128)(2,1)}, u32[]{:S(2)}) %copy-start.4) | copy-done | bytes 2097176
  88.8 6.0 %queries.1 = bf16[4,512,256]{2,1,0:T(8,128)(2,1)S(1)} custom-call(bf16[3,512,2048]{2,1,0:T(8,128)(2,1)S(1)} %copy-done.2, bf16[1,512,2048]{2,1,0:T(8,128)(2,1)S(1)} %copy-done.4, bf16[2048,256]{1,0:T(8,128)(2,1)S(1)} %copy-done.7, f32[1,128]{1,0:T(1,128)S(1)} %bitcast.70, f32[4,512,128]{2,1,0:T(8,128)S(1)} %get-tuple-element.47.cos, ...), custom_call_target="tpu_custom_call" | custom-call | flops 2147483648 | bytes 12582912 | tf_op jit(solution)/shard_map/queries/pallas_call | solution.py:230
  94.8 10.9 %attend.1 = bf16[8,264,256]{2,1,0:T(8,128)(2,1)S(1)} custom-call(s32[8]{0:T(128)S(1)} %select_reduce_fusion.2.piece_of, s32[8]{0:T(128)S(1)} %add.158.ctx_of, s32[8]{0:T(128)S(1)} %and_select_fusion.4.low, s32[4]{0:T(128)S(1)} %bitcast_subtract_fusion.starts, bf16[8,256,256]{2,1,0:T(8,128)(2,1)S(1)} %bitcast.58, bf16[2048,128]{1,0:T(8,128)(2,1)S(1)} %copy-done.20, ...), custom_call_target="tpu_custom_call" | custom-call | flops 4294967296 | bytes 4194304 | tf_op jit(solution)/shard_map/attend/pallas_call | solution.py:280
  105.7 2.7 %collective-permute-start.10 = (bf16[2,2,264,256]{3,2,1,0:T(8,128)(2,1)S(1)}, bf16[2,2,264,256]{3,2,1,0:T(8,128)(2,1)S(1)}, u32[]{:S(2)}, u32[]{:S(2)}) collective-permute-start(bf16[2,2,264,256]{3,2,1,0:T(8,128)(2,1)S(1)} %bitcast.71), channel_id=1, source_target_pairs={{0,96},{32,0},{64,32},{96,64},{1,97},{33,1},{65,33},{97,65},{2,98}... | collective-permute-start | bytes 1622024 | tf_op jit(solution)/shard_map/ppermute | solution.py:24
  108.6 0.8 collective-permute-start.9
  109.4 10.4 %collective-permute-done.10 = bf16[2,2,264,256]{3,2,1,0:T(8,128)(2,1)S(1)} collective-permute-done((bf16[2,2,264,256]{3,2,1,0:T(8,128)(2,1)S(1)}, bf16[2,2,264,256]{3,2,1,0:T(8,128)(2,1)S(1)}, u32[]{:S(2)}, u32[]{:S(2)}) %collective-permute-start.10) | collective-permute-done | bytes 540704 | tf_op jit(solution)/shard_map/ppermute | solution.py:24
  119.8 3.4 %collective-permute-start.14 = (bf16[2,264,256]{2,1,0:T(8,128)(2,1)S(1)}, bf16[2,264,256]{2,1,0:T(8,128)(2,1)S(1)}, u32[]{:S(2)}, u32[]{:S(2)}) collective-permute-start(bf16[2,264,256]{2,1,0:T(8,128)(2,1)S(1)} %slice_bitcast_fusion), channel_id=1, source_target_pairs={{0,96},{32,0},{64,32},{96,64},{1,97},{33,1},{65,33},{97,65},{2,98}... | collective-permute-start | bytes 811016 | tf_op jit(solution)/shard_map/ppermute | solution.py:24
  123.3 1.6 %collective-permute-start.13 = (bf16[264,256]{1,0:T(8,128)(2,1)S(1)}, bf16[264,256]{1,0:T(8,128)(2,1)S(1)}, u32[]{:S(2)}, u32[]{:S(2)}) collective-permute-start(bf16[264,256]{1,0:T(8,128)(2,1)S(1)} %get-tuple-element.42), channel_id=1, source_target_pairs={{0,16},{16,0},{1,17},{17,1},{2,18},{18,2},{3,19},{19,3},{4,20},{20... | collective-permute-start | bytes 405512 | tf_op jit(solution)/shard_map/ppermute | solution.py:24
  125.0 3.4 %collective-permute-done.14 = bf16[2,264,256]{2,1,0:T(8,128)(2,1)S(1)} collective-permute-done((bf16[2,264,256]{2,1,0:T(8,128)(2,1)S(1)}, bf16[2,264,256]{2,1,0:T(8,128)(2,1)S(1)}, u32[]{:S(2)}, u32[]{:S(2)}) %collective-permute-start.14) | collective-permute-done | bytes 270368 | tf_op jit(solution)/shard_map/ppermute | solution.py:24
  128.4 1.7 %collective-permute-start.15 = (bf16[264,256]{1,0:T(8,128)(2,1)S(1)}, bf16[264,256]{1,0:T(8,128)(2,1)S(1)}, u32[]{:S(2)}, u32[]{:S(2)}) collective-permute-start(bf16[264,256]{1,0:T(8,128)(2,1)S(1)} %get-tuple-element.40), channel_id=1, source_target_pairs={{0,16},{16,0},{1,17},{17,1},{2,18},{18,2},{3,19},{19,3},{4,20},{20... | collective-permute-start | bytes 405512 | tf_op jit(solution)/shard_map/ppermute | solution.py:24
  130.1 1.0 collective-permute-done.15
  131.1 1.6 %spread.1 = (bf16[256,2048]{1,0:T(8,128)(2,1)}, f32[8,8,128]{2,1,0:T(8,128)S(1)}) custom-call(s32[8]{0:T(128)S(1)} %add.158.ctx_of, bf16[1,264,256]{2,1,0:T(8,128)(2,1)S(1)} %get-tuple-element.37.refs_0_, bf16[1,264,256]{2,1,0:T(8,128)(2,1)S(1)} %bitcast.60, bf16[1,264,256]{2,1,0:T(8,128)(2,1)S(1)} %get-tuple-element.39.refs_2_, ...), custom_call_target="tpu_custom_call" | custom-call | bytes 2097152 | tf_op jit(solution)/shard_map/spread/pallas_call | solution.py:335
  132.8 0.2 copy.28
  133.1 4.2 %fill_cache.1 = bf16[512,2048]{1,0:T(8,128)(2,1)} custom-call(s32[1,512]{1,0:T(1,128)S(1)} %reshape.344.slots, bf16[8,512,256]{2,1,0:T(8,128)(2,1)} %bitcast.33.got), custom_call_target="tpu_custom_call" | custom-call | flops 1073741824 | bytes 4194304 | tf_op jit(solution)/shard_map/fill_cache/pallas_call | solution.py:310
  (105 shorter events, 2.4 us)
Async XLA Ops:
  0.6 17.0 %copy-start = (s32[16,8]{0,1:T(8,128)S(1)}, s32[16,8]{0,1:T(8,128)}, u32[]{:S(2)}) copy-start(s32[16,8]{0,1:T(8,128)} %param.20) | copy-start | bytes 1540
  0.6 6.8 %copy-start.16 = (s32[1,1,256]{2,1,0:T(1,128)S(1)}, s32[1,1,256]{2,1,0:T(1,128)}, u32[]{:S(2)}) copy-start(s32[1,1,256]{2,1,0:T(1,128)} %param.21) | copy-start | bytes 3076
  0.7 6.8 %copy-start.24 = (s32[1,1,256]{2,1,0:T(1,128)S(1)}, s32[1,1,256]{2,1,0:T(1,128)}, u32[]{:S(2)}) copy-start(s32[1,1,256]{2,1,0:T(1,128)} %param.22) | copy-start | bytes 3076
  0.7 1.2 copy-start.8
  1.9 0.7 copy-start.15
  2.6 5.4 %copy-start.11 = (bf16[128,256]{1,0:T(8,128)(2,1)S(1)}, bf16[128,256]{1,0:T(8,128)(2,1)}, u32[]{:S(2)}) copy-start(bf16[128,256]{1,0:T(8,128)(2,1)} %a.1) | copy-start | bytes 196612
  2.6 5.4 %copy-start.12 = (bf16[128,128]{1,0:T(8,128)(2,1)S(1)}, bf16[128,128]{1,0:T(8,128)(2,1)}, u32[]{:S(2)}) copy-start(bf16[128,128]{1,0:T(8,128)(2,1)} %b.1) | copy-start | bytes 98308
  2.6 5.4 %copy-start.13 = (bf16[128,128]{1,0:T(8,128)(2,1)S(1)}, bf16[128,128]{1,0:T(8,128)(2,1)}, u32[]{:S(2)}) copy-start(bf16[128,128]{1,0:T(8,128)(2,1)} %c.1) | copy-start | bytes 98308
  2.7 27.2 %collective-permute-start.3 = (bf16[264,2048]{1,0:T(8,128)(2,1)S(1)}, bf16[264,2048]{1,0:T(8,128)(2,1)}, u32[]{:S(2)}, u32[]{:S(2)}) collective-permute-start(bf16[264,2048]{1,0:T(8,128)(2,1)S(1)} %pack.1.refs_0_), channel_id=1, source_target_pairs={{0,32},{32,64},{64,96},{96,0},{1,33},{33,65},{65,97},{97,1},{2,34}... | collective-permute-start | bytes 3244040 | tf_op jit(solution)/shard_map/ppermute | solution.py:24
  4.9 26.1 %collective-permute-start.1 = (bf16[264,2048]{1,0:T(8,128)(2,1)S(1)}, bf16[264,2048]{1,0:T(8,128)(2,1)}, u32[]{:S(2)}, u32[]{:S(2)}) collective-permute-start(bf16[264,2048]{1,0:T(8,128)(2,1)S(1)} %pack.1.refs_0_), channel_id=1, source_target_pairs={{0,96},{32,0},{64,32},{96,64},{1,97},{33,1},{65,33},{97,65},{2,98}... | collective-permute-start | bytes 3244040 | tf_op jit(solution)/shard_map/ppermute | solution.py:24
  6.4 45.7 %collective-permute-start = (bf16[264,2048]{1,0:T(8,128)(2,1)S(1)}, bf16[264,2048]{1,0:T(8,128)(2,1)}, u32[]{:S(2)}, u32[]{:S(2)}) collective-permute-start(bf16[264,2048]{1,0:T(8,128)(2,1)S(1)} %pack.1.refs_0_), channel_id=1, source_target_pairs={{0,16},{16,0},{1,17},{17,1},{2,18},{18,2},{3,19},{19,3},{4,20},{20... | collective-permute-start | bytes 3244040 | tf_op jit(solution)/shard_map/ppermute | solution.py:24
  9.6 7.9 %copy-start.25 = (s32[4]{0:T(128)S(1)}, s32[4]{0:T(128)}, u32[]{:S(2)}) copy-start(s32[4]{0:T(128)} %constant.122.clone) | copy-start | bytes 52
  9.6 8.6 %copy-start.23 = (s32[16,4]{0,1:T(4,128)S(1)}, s32[16,4]{0,1:T(4,128)}, u32[]{:S(2)}) copy-start(s32[16,4]{0,1:T(4,128)} %param.19) | copy-start | bytes 772
  9.7 38.4 %all-to-all-start = ((bf16[16,136,512]{2,1,0:T(8,128)(2,1)}), bf16[16,136,512]{2,1,0:T(8,128)(2,1)}, u32[]{:S(2)}, u32[]{:S(2)}) async-start(bf16[16,136,512]{2,1,0:T(8,128)(2,1)} %spread_weights.1), calls=%async_computation | async-start | bytes 4456448 | tf_op jit(solution)/shard_map/all_to_all | solution.py:385
  31.0 13.4 %collective-permute-start.6 = (bf16[128,2048]{1,0:T(8,128)(2,1)S(1)}, bf16[128,2048]{1,0:T(8,128)(2,1)}, u32[]{:S(2)}, u32[]{:S(2)}) collective-permute-start(bf16[128,2048]{1,0:T(8,128)(2,1)S(1)} %slice.87), channel_id=1, source_target_pairs={{0,32},{32,64},{64,96},{96,0},{1,33},{33,65},{65,97},{97,1},{2,34}... | collective-permute-start | bytes 1572872 | tf_op jit(solution)/shard_map/ppermute | solution.py:24
  32.1 14.5 %collective-permute-start.5 = (bf16[136,2048]{1,0:T(8,128)(2,1)S(1)}, bf16[136,2048]{1,0:T(8,128)(2,1)}, u32[]{:S(2)}, u32[]{:S(2)}) collective-permute-start(bf16[136,2048]{1,0:T(8,128)(2,1)S(1)} %slice.86), channel_id=1, source_target_pairs={{0,96},{32,0},{64,32},{96,64},{1,97},{33,1},{65,33},{97,65},{2,98}... | collective-permute-start | bytes 1671176 | tf_op jit(solution)/shard_map/ppermute | solution.py:24
  34.9 17.3 %collective-permute-start.4 = (bf16[264,2048]{1,0:T(8,128)(2,1)}, bf16[264,2048]{1,0:T(8,128)(2,1)}, u32[]{:S(2)}, u32[]{:S(2)}) collective-permute-start(bf16[264,2048]{1,0:T(8,128)(2,1)} %collective-permute-done.3.refs_4_), channel_id=1, source_target_pairs={{0,16},{16,0},{1,17},{17,1},{2,18},{18,2},{3,19},{19,3},{4,20},{20... | collective-permute-start | bytes 3244040 | tf_op jit(solution)/shard_map/ppermute | solution.py:24
  36.8 15.4 %collective-permute-start.2 = (bf16[264,2048]{1,0:T(8,128)(2,1)}, bf16[264,2048]{1,0:T(8,128)(2,1)}, u32[]{:S(2)}, u32[]{:S(2)}) collective-permute-start(bf16[264,2048]{1,0:T(8,128)(2,1)} %collective-permute-done.1.refs_2_), channel_id=1, source_target_pairs={{0,16},{16,0},{1,17},{17,1},{2,18},{18,2},{3,19},{19,3},{4,20},{20... | collective-permute-start | bytes 3244040 | tf_op jit(solution)/shard_map/ppermute | solution.py:24
  44.4 13.1 %collective-permute-start.8 = (bf16[128,2048]{1,0:T(8,128)(2,1)}, bf16[128,2048]{1,0:T(8,128)(2,1)}, u32[]{:S(2)}, u32[]{:S(2)}) collective-permute-start(bf16[128,2048]{1,0:T(8,128)(2,1)} %collective-permute-done.6.refs_1_), channel_id=1, source_target_pairs={{0,16},{16,0},{1,17},{17,1},{2,18},{18,2},{3,19},{19,3},{4,20},{20... | collective-permute-start | bytes 1572872 | tf_op jit(solution)/shard_map/ppermute | solution.py:24
  46.7 10.8 %collective-permute-start.7 = (bf16[136,2048]{1,0:T(8,128)(2,1)}, bf16[136,2048]{1,0:T(8,128)(2,1)}, u32[]{:S(2)}, u32[]{:S(2)}) collective-permute-start(bf16[136,2048]{1,0:T(8,128)(2,1)} %collective-permute-done.5.refs_0_), channel_id=1, source_target_pairs={{0,16},{16,0},{1,17},{17,1},{2,18},{18,2},{3,19},{19,3},{4,20},{20... | collective-permute-start | bytes 1671176 | tf_op jit(solution)/shard_map/ppermute | solution.py:24
  47.8 4.4 %copy-start.14 = (f32[2048]{0:T(1024)S(1)}, f32[2048]{0:T(1024)}, u32[]{:S(2)}) copy-start(f32[2048]{0:T(1024)} %param.13) | copy-start | bytes 24580
  49.9 1.0 copy-start.6
  50.9 1.0 copy-start.9
  57.4 2.6 %copy-start.10 = (bf16[2048,256]{1,0:T(8,128)(2,1)S(1)}, bf16[2048,256]{1,0:T(8,128)(2,1)}, u32[]{:S(2)}) copy-start(bf16[2048,256]{1,0:T(8,128)(2,1)} %copy-done.9) | copy-start | bytes 3145732
  57.4 2.6 %copy-start.17 = (f32[128]{0:T(128)S(1)}, f32[128]{0:T(128)}, u32[]{:S(2)}) copy-start(f32[128]{0:T(128)} %param.18) | copy-start | bytes 1540
  60.0 8.0 %copy-start.3 = (bf16[1,512,2048]{2,1,0:T(8,128)(2,1)}, bf16[1,512,2048]{2,1,0:T(8,128)(2,1)S(1)}, u32[]{:S(2)}) copy-start(bf16[1,512,2048]{2,1,0:T(8,128)(2,1)S(1)} %get-tuple-element.18.x_b) | copy-start | bytes 6291460
  68.0 2.6 %copy-start.1 = (bf16[3,512,2048]{2,1,0:T(8,128)(2,1)}, bf16[3,512,2048]{2,1,0:T(8,128)(2,1)S(1)}, u32[]{:S(2)}) copy-start(bf16[3,512,2048]{2,1,0:T(8,128)(2,1)S(1)} %get-tuple-element.24.x_a) | copy-start | bytes 18874372
  70.6 1.4 %copy-start.5 = (bf16[128,32,256]{2,1,0:T(8,128)(2,1)}, bf16[128,32,256]{2,1,0:T(8,128)(2,1)S(1)}, u32[]{:S(2)}) copy-start(bf16[128,32,256]{2,1,0:T(8,128)(2,1)S(1)} %get-tuple-element.31) | copy-start | bytes 6291460
  72.0 0.8 copy-start.19
  72.8 0.8 copy-start.21
  73.6 10.8 %copy-start.7 = (bf16[2048,256]{1,0:T(8,128)(2,1)S(1)}, bf16[2048,256]{1,0:T(8,128)(2,1)}, u32[]{:S(2)}) copy-start(bf16[2048,256]{1,0:T(8,128)(2,1)} %copy-done.6) | copy-start | bytes 3145732
  73.6 10.8 %copy-start.18 = (f32[128]{0:T(128)S(1)}, f32[128]{0:T(128)}, u32[]{:S(2)}) copy-start(f32[128]{0:T(128)} %param.17) | copy-start | bytes 1540
  73.6 59.5 %all-to-all-start.1 = ((bf16[128,32,256]{2,1,0:T(8,128)(2,1)}), bf16[128,32,256]{2,1,0:T(8,128)(2,1)}, u32[]{:S(2)}, u32[]{:S(2)}) async-start(bf16[128,32,256]{2,1,0:T(8,128)(2,1)} %copy-done.5), calls=%async_computation.1 | async-start | bytes 4194304 | tf_op jit(solution)/shard_map/all_to_all | solution.py:421
  84.4 2.8 %copy-start.2 = (bf16[3,512,2048]{2,1,0:T(8,128)(2,1)S(1)}, bf16[3,512,2048]{2,1,0:T(8,128)(2,1)}, u32[]{:S(2)}) copy-start(bf16[3,512,2048]{2,1,0:T(8,128)(2,1)} %copy-done.1) | copy-start | bytes 18874372
  87.2 1.6 %copy-start.4 = (bf16[1,512,2048]{2,1,0:T(8,128)(2,1)S(1)}, bf16[1,512,2048]{2,1,0:T(8,128)(2,1)}, u32[]{:S(2)}) copy-start(bf16[1,512,2048]{2,1,0:T(8,128)(2,1)} %copy-done.3) | copy-start | bytes 6291460
  88.8 6.0 %copy-start.20 = (bf16[2048,128]{1,0:T(8,128)(2,1)S(1)}, bf16[2048,128]{1,0:T(8,128)(2,1)}, u32[]{:S(2)}) copy-start(bf16[2048,128]{1,0:T(8,128)(2,1)} %copy-done.19) | copy-start | bytes 1572868
  88.8 6.0 %copy-start.22 = (bf16[2048,128]{1,0:T(8,128)(2,1)S(1)}, bf16[2048,128]{1,0:T(8,128)(2,1)}, u32[]{:S(2)}) copy-start(bf16[2048,128]{1,0:T(8,128)(2,1)} %copy-done.21) | copy-start | bytes 1572868
  105.7 14.1 %collective-permute-start.10 = (bf16[2,2,264,256]{3,2,1,0:T(8,128)(2,1)S(1)}, bf16[2,2,264,256]{3,2,1,0:T(8,128)(2,1)S(1)}, u32[]{:S(2)}, u32[]{:S(2)}) collective-permute-start(bf16[2,2,264,256]{3,2,1,0:T(8,128)(2,1)S(1)} %bitcast.71), channel_id=1, source_target_pairs={{0,96},{32,0},{64,32},{96,64},{1,97},{33,1},{65,33},{97,65},{2,98}... | collective-permute-start | bytes 1622024 | tf_op jit(solution)/shard_map/ppermute | solution.py:24
  108.5 14.8 %collective-permute-start.12 = (bf16[2,264,256]{2,1,0:T(8,128)(2,1)S(1)}, bf16[2,264,256]{2,1,0:T(8,128)(2,1)S(1)}, u32[]{:S(2)}, u32[]{:S(2)}) collective-permute-start(bf16[2,264,256]{2,1,0:T(8,128)(2,1)S(1)} %slice.93), channel_id=1, source_target_pairs={{0,32},{32,64},{64,96},{96,0},{1,33},{33,65},{65,97},{97,1},{2,34}... | collective-permute-start | bytes 811016 | tf_op jit(solution)/shard_map/ppermute | solution.py:24
  108.6 21.5 %collective-permute-start.9 = (bf16[264,256]{1,0:T(8,128)(2,1)S(1)}, bf16[264,256]{1,0:T(8,128)(2,1)S(1)}, u32[]{:S(2)}, u32[]{:S(2)}) collective-permute-start(bf16[264,256]{1,0:T(8,128)(2,1)S(1)} %get-tuple-element.36), channel_id=1, source_target_pairs={{0,16},{16,0},{1,17},{17,1},{2,18},{18,2},{3,19},{19,3},{4,20},{20... | collective-permute-start | bytes 405512 | tf_op jit(solution)/shard_map/ppermute | solution.py:24
  119.8 8.5 %collective-permute-start.14 = (bf16[2,264,256]{2,1,0:T(8,128)(2,1)S(1)}, bf16[2,264,256]{2,1,0:T(8,128)(2,1)S(1)}, u32[]{:S(2)}, u32[]{:S(2)}) collective-permute-start(bf16[2,264,256]{2,1,0:T(8,128)(2,1)S(1)} %slice_bitcast_fusion), channel_id=1, source_target_pairs={{0,96},{32,0},{64,32},{96,64},{1,97},{33,1},{65,33},{97,65},{2,98}... | collective-permute-start | bytes 811016 | tf_op jit(solution)/shard_map/ppermute | solution.py:24
  123.3 6.8 %collective-permute-start.13 = (bf16[264,256]{1,0:T(8,128)(2,1)S(1)}, bf16[264,256]{1,0:T(8,128)(2,1)S(1)}, u32[]{:S(2)}, u32[]{:S(2)}) collective-permute-start(bf16[264,256]{1,0:T(8,128)(2,1)S(1)} %get-tuple-element.42), channel_id=1, source_target_pairs={{0,16},{16,0},{1,17},{17,1},{2,18},{18,2},{3,19},{19,3},{4,20},{20... | collective-permute-start | bytes 405512 | tf_op jit(solution)/shard_map/ppermute | solution.py:24
  124.9 5.2 %collective-permute-start.11 = (bf16[264,256]{1,0:T(8,128)(2,1)S(1)}, bf16[264,256]{1,0:T(8,128)(2,1)S(1)}, u32[]{:S(2)}, u32[]{:S(2)}) collective-permute-start(bf16[264,256]{1,0:T(8,128)(2,1)S(1)} %get-tuple-element.38), channel_id=1, source_target_pairs={{0,16},{16,0},{1,17},{17,1},{2,18},{18,2},{3,19},{19,3},{4,20},{20... | collective-permute-start | bytes 405512 | tf_op jit(solution)/shard_map/ppermute | solution.py:24
  128.4 2.7 %collective-permute-start.15 = (bf16[264,256]{1,0:T(8,128)(2,1)S(1)}, bf16[264,256]{1,0:T(8,128)(2,1)S(1)}, u32[]{:S(2)}, u32[]{:S(2)}) collective-permute-start(bf16[264,256]{1,0:T(8,128)(2,1)S(1)} %get-tuple-element.40), channel_id=1, source_target_pairs={{0,16},{16,0},{1,17},{17,1},{2,18},{18,2},{3,19},{19,3},{4,20},{20... | collective-permute-start | bytes 405512 | tf_op jit(solution)/shard_map/ppermute | solution.py:24

commit v2 on v1

v2 whole, which is shorter than its diff:
```python
import math

import jax
import jax.numpy as jnp
from jax import lax
from jax.experimental import pallas as pl
from jax.experimental.pallas import tpu as pltpu
from jax.sharding import Mesh, PartitionSpec as P

HEAD = 128
TOK = 256
EPSILON = 1e-06
THETA = 1000000.0
NEG_BIG = -1e30
MOST = 4
MIB = 1 << 20
ROUTE = 8
CTX = ("y", "core")
FSDP = ("x", "z")


def shift(value, axis, by):
    size = lax.axis_size(axis)
    return lax.ppermute(value, axis, [(i, (i + by) % size) for i in range(size)])


def norm_rope(raw, gain, cos, sin):
    factor = lax.rsqrt(jnp.mean(raw * raw, axis=-1, keepdims=True) + EPSILON)
    normal = raw * factor * gain
    return (normal * cos + pltpu.roll(normal, HEAD // 2, 1) * sin).astype(jnp.bfloat16)


def call(kernel, out_shape, specs, outs, mib, cost, name, scratch=(), grid=(), maps=()):
    flops, moved = cost
    return pl.pallas_call(
        kernel,
        grid_spec=pltpu.PrefetchScalarGridSpec(
            num_scalar_prefetch=len(maps),
            grid=grid,
            in_specs=specs,
            out_specs=outs,
            scratch_shapes=scratch,
        ),
        out_shape=out_shape,
        compiler_params=pltpu.CompilerParams(vmem_limit_bytes=mib * MIB),
        cost_estimate=pl.CostEstimate(flops=flops, bytes_accessed=moved * MIB, transcendentals=0),
        name=name,
    )


def shape(*dims, dtype=jnp.bfloat16):
    return jax.ShapeDtypeStruct(dims, dtype)


WHOLE = pl.BlockSpec(memory_space=pltpu.VMEM)
FAR = pl.BlockSpec(memory_space=pltpu.HBM)


def pack_kernel(hidden, own_hbm, gain_hbm, out, x, own, gain, sems):
    first = pltpu.make_async_copy(own_hbm, own, sems.at[0])
    move = pltpu.make_async_copy(hidden, x, sems.at[1])
    last = pltpu.make_async_copy(gain_hbm, gain, sems.at[2])
    first.start()
    move.start()
    last.start()
    first.wait()
    row = own[...].astype(jnp.float32)
    column = jnp.transpose(jnp.broadcast_to(row, (ROUTE, TOK)))[:, 0:1]
    token = lax.broadcasted_iota(jnp.int32, (TOK, TOK), 0)
    other = lax.broadcasted_iota(jnp.int32, (TOK, TOK), 1)
    same = (column == row) & (token < other)
    rank = jnp.sum(same.astype(jnp.float32), axis=0, keepdims=True)
    out[TOK:, :] = jnp.zeros((ROUTE, out.shape[1]), out.dtype)
    which = lax.broadcasted_iota(jnp.int32, (ROUTE, TOK), 0)
    lead = jnp.where(which == 0, row, jnp.where(which == 1, rank, 0.0))
    out[TOK:, 0:TOK] = lead.astype(out.dtype)
    move.wait()
    last.wait()
    for i in range(0, TOK, 128):
        part = x[i : i + 128, :].astype(jnp.float32)
        factor = lax.rsqrt(jnp.mean(part * part, axis=-1, keepdims=True) + EPSILON)
        out[i : i + 128, :] = (part * factor * gain[...]).astype(out.dtype)


def pack(hidden, own, gain):
    return call(
        pack_kernel,
        shape(TOK + ROUTE, 2048),
        [FAR, FAR, FAR],
        WHOLE,
        58,
        (0, 2),
        "pack",
        [
            pltpu.VMEM((TOK, 2048), jnp.bfloat16),
            pltpu.VMEM((1, TOK), jnp.int32),
            pltpu.VMEM((1, 2048), jnp.float32),
            pltpu.SemaphoreType.DMA((3,)),
        ],
    )(hidden, own, gain)


def spread_weights_kernel(a, b, c, routes, out, part, sems):
    moves = [
        pltpu.make_async_copy(a, part.at[:, pl.ds(0, 2 * HEAD)], sems.at[0]),
        pltpu.make_async_copy(b, part.at[:, pl.ds(2 * HEAD, HEAD)], sems.at[1]),
        pltpu.make_async_copy(c, part.at[:, pl.ds(3 * HEAD, HEAD)], sems.at[2]),
    ]
    for move in moves:
        move.start()
    for i in range(16):
        out[i, 128:, 0:HEAD] = routes[i]
        out[i, 128:, HEAD:] = jnp.zeros((ROUTE, 3 * HEAD), out.dtype)
    for move in moves:
        move.wait()
    for i in range(16):
        out[i, 0:128, :] = part[...]


def spread_weights(a, b, c, routes):
    return call(
        spread_weights_kernel,
        shape(16, 128 + ROUTE, 4 * HEAD),
        [FAR, FAR, FAR, WHOLE],
        WHOLE,
        6,
        (0, 3),
        "spread_weights",
        [pltpu.VMEM((128, 4 * HEAD), jnp.bfloat16), pltpu.SemaphoreType.DMA((3,))],
    )(a, b, c, routes)


def data_rows(ref):
    return ref.shape[0] - ref.shape[0] % 16


def take_weights(got, part, out):
    for i in range(16):
        out[i * 128 : (i + 1) * 128, :] = got[i, 0:128, part]


def keys(y_of_pair, piece_of, core, pairs, w, gain, cos, sin):
    count = sum(len(p) for p in pairs)

    def kernel(ys, piece, core_ref, *refs):
        w_ref, gain_ref, cos_ref, sin_ref, k_hbm, v_hbm, b_hbm = refs[count : count + 7]
        w_kv, kv, k_out, v_out, b_out, sems = refs[count + 7 :]
        step = pl.program_id(0)

        def send(i):
            at = pl.multiple_of(ys[i] * 8, 8)
            return pltpu.make_async_copy(b_out.at[i], b_hbm.at[:, pl.ds(at, 8), :], sems.at[i])

        @pl.when(step == 0)
        def _():
            take_weights(w_ref, slice(2 * HEAD, 4 * HEAD), w_kv)

        def go(part):
            at = 0
            codes = []
            for ref in part:
                rows = data_rows(ref)
                raw = jnp.dot(ref[0:rows, :], w_kv[...], preferred_element_type=jnp.float32)
                put = slice(at, at + rows)
                kv[put, :HEAD] = norm_rope(
                    raw[:, :HEAD], gain_ref[...], cos_ref[0, put, :], sin_ref[0, put, :]
                )
                kv[put, HEAD:] = raw[:, HEAD:].astype(jnp.bfloat16)
                if rows < ref.shape[0]:
                    lead = ref[rows:, 0:TOK].astype(jnp.float32)
                    side = len(codes)
                    mine = core_ref[0] + side - 2 * core_ref[0] * side
                    codes.append((lead[0:1] * 8 + lead[1:2]).astype(jnp.int32) + mine * MOST)
                at += rows
            place = lax.broadcasted_iota(jnp.int32, (8 * 128, 2 * TOK), 0)
            pick = (place == jnp.concatenate(codes, axis=1)).astype(jnp.bfloat16)
            got = jnp.dot(pick, kv[...], preferred_element_type=jnp.float32)
            b_out[step] = got.reshape(128, 8, 2 * HEAD).astype(jnp.bfloat16)
            send(step).start()
            for side in range(2):
                to = pl.ds(pl.multiple_of(piece[2 * step + side] * TOK, TOK), TOK)
                k_out[to, :] = kv[side * TOK : (side + 1) * TOK, :HEAD]
                v_out[to, :] = kv[side * TOK : (side + 1) * TOK, HEAD:]

        at = 0
        for i, p in enumerate(pairs):
            pl.when(step == i)(lambda part=refs[at : at + len(p)]: go(part))
            at += len(p)

        @pl.when(step == 3)
        def _():
            last = [
                pltpu.make_async_copy(k_out, k_hbm, sems.at[4]),
                pltpu.make_async_copy(v_out, v_hbm, sems.at[5]),
            ]
            for move in last:
                move.start()
            for i in range(4):
                send(i).wait()
            for move in last:
                move.wait()

    maps = y_of_pair, piece_of, core
    table = pl.BlockSpec((1, 2 * TOK, HEAD), lambda i, *_: (i, 0, 0))
    return call(
        kernel,
        [
            pltpu.HBM((8 * TOK, HEAD), jnp.bfloat16),
            pltpu.HBM((8 * TOK, HEAD), jnp.bfloat16),
            pltpu.HBM((128, 32, 2 * HEAD), jnp.bfloat16),
        ],
        [WHOLE] * (count + 2) + [table] * 2,
        [FAR] * 3,
        14,
        (2 * 2048 * 2048 * 256, 12),
        "keys",
        [
            pltpu.VMEM((2048, 2 * HEAD), jnp.bfloat16),
            pltpu.VMEM((2 * TOK, 2 * HEAD), jnp.bfloat16),
            pltpu.VMEM((8 * TOK, HEAD), jnp.bfloat16),
            pltpu.VMEM((8 * TOK, HEAD), jnp.bfloat16),
            pltpu.VMEM((4, 128, 8, 2 * HEAD), jnp.bfloat16),
            pltpu.SemaphoreType.DMA((6,)),
        ],
        (4,),
        maps,
    )(*maps, *(x for p in pairs for x in p), w, gain, cos, sin)


def attend(first, pieces, piece_of, ctx_of, low, starts, w, gain, cos, sin, k, v, leads):
    count = sum(len(p) for p in pieces)

    def kernel(piece, ctx, lows, begins, *refs):
        w_ref, gain_ref, cos_ref, sin_ref, k_hbm, v_hbm, lead, out = refs[count : count + 8]
        w_q, both, keys_ref, values, sems = refs[count + 8 :]
        step = pl.program_id(0)
        moves = [
            pltpu.make_async_copy(k_hbm, keys_ref, sems.at[0]),
            pltpu.make_async_copy(v_hbm, values, sems.at[1]),
        ]

        @pl.when(step == 0)
        def _():
            for move in moves:
                move.start()
            take_weights(w_ref, slice(0, 2 * HEAD), w_q)

        def query(part):
            at = 0
            for ref in part:
                rows = data_rows(ref)
                raw = jnp.dot(ref[0:rows, :], w_q[...], preferred_element_type=jnp.float32)
                put = slice(at, at + rows)
                for h in range(2):
                    both[h * TOK + at : h * TOK + at + rows, :] = norm_rope(
                        raw[:, h * HEAD : (h + 1) * HEAD],
                        gain_ref[...],
                        cos_ref[0, put, :],
                        sin_ref[0, put, :],
                    )
                at += rows

        at = 0
        for i, p in enumerate(pieces):
            pl.when(step == i)(lambda part=refs[at : at + len(p)]: query(part))
            at += len(p)

        @pl.when(step == 0)
        def _():
            for move in moves:
                move.wait()

        p = piece[first + step]
        lo = lows[p]
        out[0, TOK:, :] = lead[0]
        place = p * TOK + lax.broadcasted_iota(jnp.int32, (TOK, 1), 0)
        begin = jnp.zeros_like(place)
        for n in range(1, 4):
            begin = jnp.where(begins[n] <= place, begins[n], begin)

        def blocks(span):
            at = pl.multiple_of(lo * TOK, TOK)
            spot = at + lax.broadcasted_iota(jnp.int32, (1, span), 1)
            seen = (spot <= place) & (spot >= begin)
            for h in range(2):
                s = lax.dot_general(
                    both[h * TOK : (h + 1) * TOK],
                    keys_ref[pl.ds(at, span), :],
                    (((1,), (1,)), ((), ())),
                    preferred_element_type=jnp.float32,
                )
                s = jnp.where(seen, s, NEG_BIG)
                top = jnp.max(s, axis=1, keepdims=True)
                e = jnp.exp((s - top) * (1.0 / math.sqrt(HEAD)))
                total = jnp.sum(e, axis=1, keepdims=True)
                mixed = jnp.dot(
                    e.astype(jnp.bfloat16),
                    values[pl.ds(at, span), :],
                    preferred_element_type=jnp.float32,
                )
                out[0, 0:TOK, h * HEAD : (h + 1) * HEAD] = (mixed / total).astype(jnp.bfloat16)

        for n in range(1, 6):
            pl.when(p + 1 - lo == n)(lambda n=n: blocks(n * TOK))

    maps = piece_of, ctx_of, low, starts
    n = len(pieces)
    table = pl.BlockSpec((1, TOK, HEAD), lambda i, *_: (first // 2 + i // 2, i % 2, 0))
    return call(
        kernel,
        shape(n, TOK + ROUTE, 2 * HEAD),
        [WHOLE] * (count + 2)
        + [table] * 2
        + [FAR] * 2
        + [pl.BlockSpec((1, ROUTE, 2 * HEAD), lambda i, p, c, *_: (c[first + i], 0, 0))],
        pl.BlockSpec((1, TOK + ROUTE, 2 * HEAD), lambda i, *_: (i, 0, 0)),
        16,
        (n * 2048 * 2048 * 128, 4),
        "attend",
        [
            pltpu.VMEM((2048, 2 * HEAD), jnp.bfloat16),
            pltpu.VMEM((2 * TOK, HEAD), jnp.bfloat16),
            pltpu.VMEM((8 * TOK, HEAD), jnp.bfloat16),
            pltpu.VMEM((8 * TOK, HEAD), jnp.bfloat16),
            pltpu.SemaphoreType.DMA((2,)),
        ],
        (n,),
        maps,
    )(
        *maps,
        *(x for p in pieces for x in p),
        w,
        gain,
        cos,
        sin,
        k,
        v,
        leads,
    )


def cache_kernel(leads, got, out, rows, in_sems):
    takes = [pltpu.make_async_copy(got.at[c], rows.at[c], in_sems.at[c]) for c in range(8)]
    for take in takes:
        take.start()
    column = lax.broadcasted_iota(jnp.int32, (HEAD, 512), 1)
    entry = lax.broadcasted_iota(jnp.int32, (HEAD, 512), 0)
    turn = (entry == jnp.bitwise_or((column >> 5) << 2, jnp.bitwise_and(column, 3))).astype(
        jnp.bfloat16
    )
    high = jnp.dot(leads[:, 0, :], turn, preferred_element_type=jnp.float32)
    low = jnp.dot(leads[:, 1, :], turn, preferred_element_type=jnp.float32)
    place = lax.broadcasted_iota(jnp.int32, (8, 512), 0)
    from_ctx = jnp.bitwise_and(lax.broadcasted_iota(jnp.int32, (8, 512), 1) >> 2, 7)
    slots = jnp.sum(
        jnp.where(place == from_ctx, high * 16 + low, 0.0), axis=0, keepdims=True
    ).astype(jnp.int32)
    pick = (lax.broadcasted_iota(jnp.int32, (512, 512), 0) == slots - 1).astype(jnp.bfloat16)
    for c in range(8):
        takes[c].wait()
        part = jnp.dot(pick, rows[c], preferred_element_type=jnp.float32).astype(jnp.bfloat16)
        out[:, c * HEAD : (c + 1) * HEAD] = part[:, :HEAD]
        out[:, (8 + c) * HEAD : (9 + c) * HEAD] = part[:, HEAD:]


def fill_cache(leads, got):
    return call(
        cache_kernel,
        shape(512, 2048),
        [WHOLE, FAR],
        WHOLE,
        10,
        (2 * 512 * 512 * 2048, 4),
        "fill_cache",
        [pltpu.VMEM((8, 512, 2 * HEAD), jnp.bfloat16), pltpu.SemaphoreType.DMA((8,))],
    )(leads, got)


def spread_kernel(ctx_of, *refs):
    out, leads = refs[-2:]
    side = 0
    for ref in refs[:-2]:
        for i in range(ref.shape[0]):
            ctx = ctx_of[side]
            to = pl.ds(pl.multiple_of(ctx * 2 * HEAD, 2 * HEAD), 2 * HEAD)
            out[:, to] = ref[i, 0:TOK]
            leads[ctx] = ref[i, TOK:, 0:HEAD]
            side += 1


def spread(ctx_of, parts):
    return call(
        spread_kernel,
        [shape(TOK, 2048), shape(8, ROUTE, HEAD)],
        [pl.BlockSpec(memory_space=pltpu.SMEM)] + [WHOLE] * len(parts),
        [WHOLE] * 2,
        6,
        (0, 2),
        "spread",
    )(ctx_of, *parts)


def choose(index, table):
    hit = index[:, None] == jnp.arange(table.shape[0], dtype=jnp.int32)[None, :]
    return jnp.sum(jnp.where(hit, table[None], 0), axis=1, dtype=jnp.int32)


def shards(
    hidden, norm_gain, w_query, w_key, w_value, q_gain, k_gain, lengths, piece_map, owner, slot
):
    y, core = lax.axis_index("y"), lax.axis_index("core")
    group = lax.axis_index(FSDP)
    own = owner[0, 0]
    offsets = jnp.array([0, 1, 3, 2], jnp.int32)

    my_pieces = lax.dynamic_index_in_dim(piece_map, group, 0, keepdims=False)
    my_lengths = lax.dynamic_index_in_dim(lengths, group, 0, keepdims=False)
    ends = jnp.cumsum(my_lengths, dtype=jnp.int32)
    starts = ends - my_lengths
    y_of_pair = ((y + offsets) % 4).astype(jnp.int32)
    core_of = jnp.stack([core, 1 - core]).astype(jnp.int32)
    ctx_of_slot = (y_of_pair[:, None] * 2 + core_of[None, :]).reshape(-1)
    piece_of_slot = choose(ctx_of_slot, my_pieces)
    eight = jnp.arange(8, dtype=jnp.int32)

    def begin_of(places):
        reached = starts[None, :] <= places.reshape(-1, 1)
        return jnp.max(jnp.where(reached, starts[None, :], 0), axis=1).reshape(places.shape)

    low = begin_of(eight * TOK) // TOK
    places = piece_of_slot[:, None] * TOK + jnp.arange(TOK, dtype=jnp.int32)[None, :]
    relative = places - begin_of(places)
    frequency = jnp.exp(jnp.arange(HEAD // 2, dtype=jnp.float32) * (-2.0 * math.log(THETA) / HEAD))
    angles = relative.astype(jnp.float32).reshape(4, 2 * TOK, 1) * frequency
    cos, sin = jnp.cos(angles), jnp.sin(angles)
    cos = jnp.concatenate([cos, cos], axis=-1)
    sin = jnp.concatenate([-sin, sin], axis=-1)

    h = pack(hidden[0, 0], own[None], norm_gain[None])
    above, below = shift(h, "y", -1), shift(h, "y", 1)
    above, below, cos, sin = lax.optimization_barrier((above, below, cos, sin))
    near, half = h, TOK // 2
    far_lo, far_hi = shift(above[:half], "y", -1), shift(below[half:], "y", 1)
    swap = lambda value: shift(value, "core", 1)
    pairs = [
        (near, swap(near)),
        (above, swap(above)),
        (below, swap(below)),
        (far_lo, far_hi, swap(far_lo), swap(far_hi)),
    ]

    token = jnp.arange(TOK, dtype=jnp.int32)
    same = (own[:, None] == own[None, :]) & (token[None, :] < token[:, None])
    rank = jnp.sum(same.astype(jnp.int32), axis=1, dtype=jnp.int32)
    spot = (own % 16) * 32 + (own // 16) * MOST + rank
    hit = spot[None, :] == jnp.arange(512, dtype=jnp.int32)[:, None]
    table = jnp.sum(jnp.where(hit, slot[0, 0][None, :] + 1, 0), axis=1, dtype=jnp.int32)
    table = table.reshape(16, 1, 32)
    table = jnp.concatenate([table // 16, table % 16], axis=1).astype(jnp.bfloat16)
    table = jnp.pad(table, ((0, 0), (0, ROUTE - 2), (0, HEAD - 32)))
    _, table = lax.optimization_barrier((h, table))
    w = spread_weights(w_query, w_key, w_value, table)
    w = lax.all_to_all(w, FSDP, split_axis=0, concat_axis=0, tiled=True)
    leads = w[:, 128:130, :32].reshape(16, 2, 8, MOST).transpose(2, 1, 0, 3).reshape(8, 2, 64)
    leads = jnp.pad(leads, ((0, 0), (0, ROUTE - 2), (0, 2 * HEAD - 64)))

    core = core.astype(jnp.int32)[None]
    k, v, buckets = keys(y_of_pair, piece_of_slot, core, pairs, w, k_gain[None], cos, sin)
    got = lax.all_to_all(buckets, CTX + FSDP, split_axis=0, concat_axis=0, tiled=True)
    maps = piece_of_slot, ctx_of_slot, low, starts
    rest = w, q_gain[None], cos, sin, k, v, leads
    far = [(far_lo, far_hi), (pairs[3][2], pairs[3][3])]
    late = attend(4, [(x,) for x in pairs[2]] + far, *maps, *rest)
    late = late.reshape(2, 2, TOK + ROUTE, 2 * HEAD)
    from_above = shift(late, "y", -1)
    mixed = attend(0, [(x,) for x in pairs[0] + pairs[1]], *maps, *rest)
    mixed = mixed.reshape(2, 2, TOK + ROUTE, 2 * HEAD)
    from_below = shift(mixed[1], "y", 1)
    from_far = shift(from_above[1], "y", -1)
    mine = [mixed[0], from_above[0], from_below, from_far]
    other = [swap(m[1]) for m in mine]
    parts = [p for m, o in zip(mine, other) for p in (m[0][None], o[None])]
    attended, leads = spread(ctx_of_slot, parts)
    cache = fill_cache(leads, got.reshape(8, 512, 2 * HEAD))
    return attended[None, None], cache


def solution(mesh):
    split = Mesh(mesh.devices.reshape(4, 2, 4, 4), (*CTX, *FSDP))
    placed = (
        P(CTX, FSDP, None, None),
        P(),
        P(FSDP, CTX),
        P(FSDP, CTX),
        P(FSDP, CTX),
        P(),
        P(),
        P(),
        P(),
        P(CTX, FSDP, None),
        P(CTX, FSDP, None),
    )
    return jax.shard_map(
        shards,
        mesh=split,
        in_specs=placed,
        out_specs=(P(CTX, FSDP, None, None), P((*CTX, *FSDP), None)),
        check_vma=False,
    )
```

time: 138 us -> 131 us (0.949)
  local copies, waits for them, and re-layouts: 17.6 us -> 12.7 us
  Pallas kernels: 41.8 us -> 38.5 us
  waiting for transfers between devices: 29.4 us -> 32.6 us
  starting transfers between devices: 41.7 us -> 39.1 us
    unnamed x58 -> x50, local copies, waits for them, and re-layouts: 14.1 us -> 9.61 us
    ppermute x16, waiting for transfers between devices: 29.1 us -> 32.6 us  [shift(): lax.ppermute(value, axis, [(i, (i + by) % size) for i in range(size)])]
    pallas_call x10 -> x7, Pallas kernels: 41.8 us -> 38.5 us  [the longest x2 18 us: attend(): call(kernel, shape(n, TOK + ROUTE, 2 * HEAD), [WHOLE] * (count + 2) + [ta...]
    ppermute x16, starting transfers between devices: 23.1 us -> 20.9 us  [shift(): lax.ppermute(value, axis, [(i, (i + by) % size) for i in range(size)])]
  transfers between devices with their start and end apart: 18 -> 18, of which waited for: 6 -> 7; matrix products, arithmetic and copies ran while one was open for 7% -> 8% of each run, Pallas kernels for 20% -> 15%
where the time goes in v2:
time: 131 us
  starting transfers between devices  39.1 us (30%)
  Pallas kernels  38.5 us (29%)
  waiting for transfers between devices  32.6 us (25%)
  local copies, waits for them, and re-layouts  12.7 us (10%)
  other arithmetic  6.57 us (5%)
    ppermute x16, waiting for transfers between devices, shift(): lax.ppermute(value, axis, [(i, (i + by) % size) for i in range(size)])  32.6 us
    ppermute x16, starting transfers between devices, shift(): lax.ppermute(value, axis, [(i, (i + by) % size) for i in range(size)])  20.9 us
    pallas_call x2, Pallas kernels, attend(): call(kernel, shape(n, TOK + ROUTE, 2 * HEAD), [WHOLE] * (count + 2) + [ta...  18 us
    all_to_all x1, starting transfers between devices, shards(): lax.all_to_all(buckets, CTX + FSDP, split_axis=0, concat_axis=0, tiled=True)  10.5 us
    pallas_call x1, Pallas kernels, keys(): call(kernel, [pltpu.HBM((8 * TOK, HEAD), jnp.bfloat16), pltpu.HBM((8 * TO...  10.1 us
    unnamed x50, local copies, waits for them, and re-layouts  9.61 us
    all_to_all x1, starting transfers between devices, shards(): w = lax.all_to_all(w, FSDP, split_axis=0, concat_axis=0, tiled=True)  7.73 us
    pallas_call x1, Pallas kernels, fill_cache(): call(cache_kernel, shape(512, 2048), [WHOLE, FAR], WHOLE, 10, (2 * 512 *...  5.73 us
  transfers between devices with their start and end apart: 18, of which 7 were waited for; matrix products, arithmetic and copies ran while one was open for 8% of the time, Pallas kernels for 15%

profile of v2, /device:TPU:1, one launch (start us, length us, event | category | flops | bytes accessed | tf_op | source)
XLA Modules:
  0.0 130.7 jit_solution(3805975453557266642)
XLA Ops:
  0.7 2.7 %pack.1.refs_0_ = bf16[264,2048]{1,0:T(8,128)(2,1)} custom-call(bf16[256,2048]{1,0:T(8,128)(2,1)} %bitcast.61, s32[1,256]{1,0:T(1,128)} %bitcast.66, f32[1,2048]{1,0:T(1,128)} %bitcast.69), custom_call_target="tpu_custom_call" | custom-call | bytes 2097152 | tf_op jit(solution)/shard_map/pack/pallas_call | solution.py:86
  3.4 2.2 %collective-permute-start.2 = (bf16[264,2048]{1,0:T(8,128)(2,1)}, bf16[264,2048]{1,0:T(8,128)(2,1)}, u32[]{:S(2)}, u32[]{:S(2)}) collective-permute-start(bf16[264,2048]{1,0:T(8,128)(2,1)} %pack.1.refs_0_), channel_id=1, source_target_pairs={{0,32},{32,64},{64,96},{96,0},{1,33},{33,65},{65,97},{97,1},{2,34}... | collective-permute-start | bytes 3244040 | tf_op jit(solution)/shard_map/ppermute | solution.py:24
  5.6 1.5 %collective-permute-start.1 = (bf16[264,2048]{1,0:T(8,128)(2,1)}, bf16[264,2048]{1,0:T(8,128)(2,1)}, u32[]{:S(2)}, u32[]{:S(2)}) collective-permute-start(bf16[264,2048]{1,0:T(8,128)(2,1)} %pack.1.refs_0_), channel_id=1, source_target_pairs={{0,96},{32,0},{64,32},{96,64},{1,97},{33,1},{65,33},{97,65},{2,98}... | collective-permute-start | bytes 3244040 | tf_op jit(solution)/shard_map/ppermute | solution.py:24
  7.2 0.2 convert_reduce_fusion
  7.4 0.2 select_reduce_fusion
  7.8 0.2 spread_weights.1
  8.0 1.4 %copy-done.6 = bf16[16,136,512]{2,1,0:T(8,128)(2,1)} copy-done((bf16[16,136,512]{2,1,0:T(8,128)(2,1)}, bf16[16,136,512]{2,1,0:T(8,128)(2,1)S(1)}, u32[]{:S(2)}) %copy-start.6) | copy-done | bytes 2228248
  9.4 7.7 %all-to-all-start = ((bf16[16,136,512]{2,1,0:T(8,128)(2,1)}), bf16[16,136,512]{2,1,0:T(8,128)(2,1)S(1)}, u32[]{:S(2)}, u32[]{:S(2)}) async-start(bf16[16,136,512]{2,1,0:T(8,128)(2,1)} %copy-done.6), calls=%async_computation | async-start | bytes 4456448 | tf_op jit(solution)/shard_map/all_to_all | solution.py:463
  17.4 0.2 dynamic-slice_reduce_fusion
  17.6 0.2 select_reduce_fusion.2.piece
  18.1 0.2 reduce-window.4
  18.4 0.1 select_reduce_fusion.1
  18.5 3.7 %fusion = (f32[4,512,64]{2,1,0:T(8,128)S(1)}, f32[4,512,64]{2,1,0:T(8,128)S(1)}, f32[4,512,64]{2,1,0:T(8,128)S(1)}) fusion(f32[64]{0:T(128)S(1)} %multiply_exponential_fusion, f32[4,512]{1,0:T(4,128)S(1)} %subtract_convert_fusion), kind=kLoop, calls=%fused_computation.6 | loop fusion | flops 262144 | bytes 1581312 | tf_op jit(solution)/shard_map/neg | solution.py:437
  22.2 1.6 %pad_maximum_fusion = (f32[4,512,128]{2,1,0:T(8,128)S(1)}, f32[4,512,128]{2,1,0:T(8,128)}) fusion(f32[4,512,64]{2,1,0:T(8,128)S(1)} %get-tuple-element.36, f32[4,512,64]{2,1,0:T(8,128)S(1)} %get-tuple-element.35, f32[4,512,64]{2,1,0:T(8,128)S(1)} %get-tuple-element.34), kind=kLoop, calls=%fused_computation.2 | loop fusion | flops 524288 | bytes 3670016 | tf_op jit(solution)/shard_map/concatenate | solution.py:436
  23.8 7.0 %collective-permute-done.2.refs_4_.refs_0_ = bf16[264,2048]{1,0:T(8,128)(2,1)} collective-permute-done((bf16[264,2048]{1,0:T(8,128)(2,1)}, bf16[264,2048]{1,0:T(8,128)(2,1)}, u32[]{:S(2)}, u32[]{:S(2)}) %collective-permute-start.2) | collective-permute-done | bytes 1081376 | tf_op jit(solution)/shard_map/ppermute | solution.py:24
  30.8 1.1 slice.53
  31.9 0.9 collective-permute-start.6
  32.8 2.1 %collective-permute-start = (bf16[264,2048]{1,0:T(8,128)(2,1)S(1)}, bf16[264,2048]{1,0:T(8,128)(2,1)S(1)}, u32[]{:S(2)}, u32[]{:S(2)}) collective-permute-start(bf16[264,2048]{1,0:T(8,128)(2,1)S(1)} %copy-done.3), channel_id=1, source_target_pairs={{0,16},{16,0},{1,17},{17,1},{2,18},{18,2},{3,19},{19,3},{4,20},{20... | collective-permute-start | bytes 3244040 | tf_op jit(solution)/shard_map/ppermute | solution.py:24
  35.0 0.5 collective-permute-start.4
  35.5 1.1 slice.52
  36.6 1.4 %collective-permute-start.5 = (bf16[128,2048]{1,0:T(8,128)(2,1)S(1)}, bf16[128,2048]{1,0:T(8,128)(2,1)}, u32[]{:S(2)}, u32[]{:S(2)}) collective-permute-start(bf16[128,2048]{1,0:T(8,128)(2,1)S(1)} %slice.52), channel_id=1, source_target_pairs={{0,96},{32,0},{64,32},{96,64},{1,97},{33,1},{65,33},{97,65},{2,98}... | collective-permute-start | bytes 1572872 | tf_op jit(solution)/shard_map/ppermute | solution.py:24
  38.0 8.0 %collective-permute-done.6.refs_7_.refs_3_ = bf16[136,2048]{1,0:T(8,128)(2,1)} collective-permute-done((bf16[136,2048]{1,0:T(8,128)(2,1)S(1)}, bf16[136,2048]{1,0:T(8,128)(2,1)}, u32[]{:S(2)}, u32[]{:S(2)}) %collective-permute-start.6) | collective-permute-done | bytes 557088 | tf_op jit(solution)/shard_map/ppermute | solution.py:24
  46.0 2.3 %collective-permute-start.8 = (bf16[136,2048]{1,0:T(8,128)(2,1)}, bf16[136,2048]{1,0:T(8,128)(2,1)}, u32[]{:S(2)}, u32[]{:S(2)}) collective-permute-start(bf16[136,2048]{1,0:T(8,128)(2,1)} %collective-permute-done.6.refs_7_.refs_3_), channel_id=1, source_target_pairs={{0,16},{16,0},{1,17},{17,1},{2,18},{18,2},{3,19},{19,3},{4,20},{20... | collective-permute-start | bytes 1671176 | tf_op jit(solution)/shard_map/ppermute | solution.py:24
  48.4 1.9 %collective-permute-done.5.refs_6_.refs_2_ = bf16[128,2048]{1,0:T(8,128)(2,1)} collective-permute-done((bf16[128,2048]{1,0:T(8,128)(2,1)S(1)}, bf16[128,2048]{1,0:T(8,128)(2,1)}, u32[]{:S(2)}, u32[]{:S(2)}) %collective-permute-start.5) | collective-permute-done | bytes 524320 | tf_op jit(solution)/shard_map/ppermute | solution.py:24
  50.3 0.8 collective-permute-start.7
  51.2 1.0 copy-done.7
  52.2 0.8 collective-permute-done.7.refs_8_.refs_4_
  53.0 1.2 copy-done.1
  54.2 1.2 copy-done.4
  55.5 1.2 copy-done.8
  56.7 10.1 %keys.1 = (bf16[2048,128]{1,0:T(8,128)(2,1)}, bf16[2048,128]{1,0:T(8,128)(2,1)}, bf16[128,32,256]{2,1,0:T(8,128)(2,1)}) custom-call(s32[4]{0:T(128)S(1)} %get-tuple-element.25.ys, s32[8]{0:T(128)S(1)} %select_reduce_fusion.2.piece, s32[1]{0:T(128)} %bitcast.core_ref, bf16[264,2048]{1,0:T(8,128)(2,1)S(1)} %copy-done.4, bf16[264,2048]{1,0:T(8,128)(2,1)S(1)} %copy-done.8, ...), custom_call_target="tpu_custom_call" | custom-call | flops 2147483648 | bytes 12582912 | tf_op jit(solution)/shard_map/keys/pallas_call | solution.py:205
  66.8 10.5 %all-to-all-start.1 = ((bf16[128,32,256]{2,1,0:T(8,128)(2,1)}), bf16[128,32,256]{2,1,0:T(8,128)(2,1)}, u32[]{:S(2)}, u32[]{:S(2)}) async-start(bf16[128,32,256]{2,1,0:T(8,128)(2,1)} %get-tuple-element.21), calls=%async_computation.1 | async-start | bytes 4194304 | tf_op jit(solution)/shard_map/all_to_all | solution.py:469
  77.5 0.1 copy.22
  77.8 1.2 copy-done.2
  79.0 1.0 copy-done.10
  80.0 1.0 copy-done.12
  81.1 9.5 %attend.3 = bf16[4,264,256]{2,1,0:T(8,128)(2,1)S(1)} custom-call(s32[8]{0:T(128)S(1)} %select_reduce_fusion.2.piece, s32[8]{0:T(128)S(1)} %add.153.ctx.ctx_of, s32[8]{0:T(128)S(1)} %and_select_fusion.4.lows, s32[4]{0:T(128)S(1)} %bitcast_subtract_fusion.begins, bf16[264,2048]{1,0:T(8,128)(2,1)} %collective-permute-done.2.refs_4_.refs_0_, ...), custom_call_target="tpu_custom_call" | custom-call | flops 2147483648 | bytes 4194304 | tf_op jit(solution)/shard_map/attend/pallas_call | solution.py:309
  90.6 3.4 %collective-permute-start.10 = (bf16[2,2,264,256]{3,2,1,0:T(8,128)(2,1)S(1)}, bf16[2,2,264,256]{3,2,1,0:T(8,128)(2,1)S(1)}, u32[]{:S(2)}, u32[]{:S(2)}) collective-permute-start(bf16[2,2,264,256]{3,2,1,0:T(8,128)(2,1)S(1)} %bitcast.53), channel_id=1, source_target_pairs={{0,96},{32,0},{64,32},{96,64},{1,97},{33,1},{65,33},{97,65},{2,98}... | collective-permute-start | bytes 1622024 | tf_op jit(solution)/shard_map/ppermute | solution.py:24
  94.0 8.5 %attend.2 = bf16[4,264,256]{2,1,0:T(8,128)(2,1)S(1)} custom-call(s32[8]{0:T(128)S(1)} %select_reduce_fusion.2.piece, s32[8]{0:T(128)S(1)} %add.153.ctx.ctx_of, s32[8]{0:T(128)S(1)} %and_select_fusion.4.lows, s32[4]{0:T(128)S(1)} %bitcast_subtract_fusion.begins, bf16[264,2048]{1,0:T(8,128)(2,1)S(1)} %copy-done.5, bf16[264,2048]{1,0:T(8,128)(2,1)S(1)} %copy-done.9, ...), custom_call_target="tpu_custom_call" | custom-call | flops 2147483648 | bytes 4194304 | tf_op jit(solution)/shard_map/attend/pallas_call | solution.py:309
  102.7 0.7 collective-permute-start.9
  103.4 9.1 %collective-permute-done.10 = bf16[2,2,264,256]{3,2,1,0:T(8,128)(2,1)S(1)} collective-permute-done((bf16[2,2,264,256]{3,2,1,0:T(8,128)(2,1)S(1)}, bf16[2,2,264,256]{3,2,1,0:T(8,128)(2,1)S(1)}, u32[]{:S(2)}, u32[]{:S(2)}) %collective-permute-start.10) | collective-permute-done | bytes 540704 | tf_op jit(solution)/shard_map/ppermute | solution.py:24
  112.5 2.8 %collective-permute-start.14 = (bf16[2,264,256]{2,1,0:T(8,128)(2,1)S(1)}, bf16[2,264,256]{2,1,0:T(8,128)(2,1)S(1)}, u32[]{:S(2)}, u32[]{:S(2)}) collective-permute-start(bf16[2,264,256]{2,1,0:T(8,128)(2,1)S(1)} %slice_bitcast_fusion), channel_id=1, source_target_pairs={{0,96},{32,0},{64,32},{96,64},{1,97},{33,1},{65,33},{97,65},{2,98}... | collective-permute-start | bytes 811016 | tf_op jit(solution)/shard_map/ppermute | solution.py:24
  115.3 0.8 collective-permute-start.13
  116.2 4.7 %collective-permute-done.14 = bf16[2,264,256]{2,1,0:T(8,128)(2,1)S(1)} collective-permute-done((bf16[2,264,256]{2,1,0:T(8,128)(2,1)S(1)}, bf16[2,264,256]{2,1,0:T(8,128)(2,1)S(1)}, u32[]{:S(2)}, u32[]{:S(2)}) %collective-permute-start.14) | collective-permute-done | bytes 270368 | tf_op jit(solution)/shard_map/ppermute | solution.py:24
  120.9 1.2 collective-permute-start.15
  122.1 1.0 collective-permute-done.15
  123.1 1.6 %spread.1 = (bf16[256,2048]{1,0:T(8,128)(2,1)}, bf16[8,8,128]{2,1,0:T(8,128)(2,1)S(1)}) custom-call(s32[8]{0:T(128)S(1)} %add.153.ctx.ctx_of, bf16[1,264,256]{2,1,0:T(8,128)(2,1)S(1)} %get-tuple-element.29.refs_0_, bf16[1,264,256]{2,1,0:T(8,128)(2,1)S(1)} %bitcast.54, bf16[1,264,256]{2,1,0:T(8,128)(2,1)S(1)} %get-tuple-element.27.refs_2_, ...), custom_call_target="tpu_custom_call" | custom-call | bytes 2097152 | tf_op jit(solution)/shard_map/spread/pallas_call | solution.py:392
  124.8 5.7 %fill_cache.1 = bf16[512,2048]{1,0:T(8,128)(2,1)} custom-call(bf16[8,8,128]{2,1,0:T(8,128)(2,1)S(1)} %get-tuple-element.20.leads, bf16[8,512,256]{2,1,0:T(8,128)(2,1)} %bitcast.29.got), custom_call_target="tpu_custom_call" | custom-call | flops 1073741824 | bytes 4194304 | tf_op jit(solution)/shard_map/fill_cache/pallas_call | solution.py:367
  (88 shorter events, 1.6 us)
Async XLA Ops:
  0.6 16.7 %copy-start = (s32[16,8]{0,1:T(8,128)S(1)}, s32[16,8]{0,1:T(8,128)}, u32[]{:S(2)}) copy-start(s32[16,8]{0,1:T(8,128)} %param.20) | copy-start | bytes 1540
  0.6 6.5 %copy-start.18 = (s32[1,1,256]{2,1,0:T(1,128)S(1)}, s32[1,1,256]{2,1,0:T(1,128)}, u32[]{:S(2)}) copy-start(s32[1,1,256]{2,1,0:T(1,128)} %param.21) | copy-start | bytes 3076
  0.7 6.5 %copy-start.20 = (s32[1,1,256]{2,1,0:T(1,128)S(1)}, s32[1,1,256]{2,1,0:T(1,128)}, u32[]{:S(2)}) copy-start(s32[1,1,256]{2,1,0:T(1,128)} %param.22) | copy-start | bytes 3076
  0.7 7.1 %copy-start.13 = (bf16[128,256]{1,0:T(8,128)(2,1)S(1)}, bf16[128,256]{1,0:T(8,128)(2,1)}, u32[]{:S(2)}) copy-start(bf16[128,256]{1,0:T(8,128)(2,1)} %a.1) | copy-start | bytes 196612
  0.7 7.1 %copy-start.14 = (bf16[128,128]{1,0:T(8,128)(2,1)S(1)}, bf16[128,128]{1,0:T(8,128)(2,1)}, u32[]{:S(2)}) copy-start(bf16[128,128]{1,0:T(8,128)(2,1)} %b.1) | copy-start | bytes 98308
  0.7 7.1 %copy-start.15 = (bf16[128,128]{1,0:T(8,128)(2,1)S(1)}, bf16[128,128]{1,0:T(8,128)(2,1)}, u32[]{:S(2)}) copy-start(bf16[128,128]{1,0:T(8,128)(2,1)} %c.1) | copy-start | bytes 98308
  3.4 27.4 %collective-permute-start.2 = (bf16[264,2048]{1,0:T(8,128)(2,1)}, bf16[264,2048]{1,0:T(8,128)(2,1)}, u32[]{:S(2)}, u32[]{:S(2)}) collective-permute-start(bf16[264,2048]{1,0:T(8,128)(2,1)} %pack.1.refs_0_), channel_id=1, source_target_pairs={{0,32},{32,64},{64,96},{96,0},{1,33},{33,65},{65,97},{97,1},{2,34}... | collective-permute-start | bytes 3244040 | tf_op jit(solution)/shard_map/ppermute | solution.py:24
  5.6 25.2 %collective-permute-start.1 = (bf16[264,2048]{1,0:T(8,128)(2,1)}, bf16[264,2048]{1,0:T(8,128)(2,1)}, u32[]{:S(2)}, u32[]{:S(2)}) collective-permute-start(bf16[264,2048]{1,0:T(8,128)(2,1)} %pack.1.refs_0_), channel_id=1, source_target_pairs={{0,96},{32,0},{64,32},{96,64},{1,97},{33,1},{65,33},{97,65},{2,98}... | collective-permute-start | bytes 3244040 | tf_op jit(solution)/shard_map/ppermute | solution.py:24
  8.0 1.4 %copy-start.6 = (bf16[16,136,512]{2,1,0:T(8,128)(2,1)}, bf16[16,136,512]{2,1,0:T(8,128)(2,1)S(1)}, u32[]{:S(2)}) copy-start(bf16[16,136,512]{2,1,0:T(8,128)(2,1)S(1)} %spread_weights.1) | copy-start | bytes 6684676
  9.4 7.8 %copy-start.21 = (s32[4]{0:T(128)S(1)}, s32[4]{0:T(128)}, u32[]{:S(2)}) copy-start(s32[4]{0:T(128)} %constant.118.clone) | copy-start | bytes 52
  9.4 8.5 %copy-start.19 = (s32[16,4]{0,1:T(4,128)S(1)}, s32[16,4]{0,1:T(4,128)}, u32[]{:S(2)}) copy-start(s32[16,4]{0,1:T(4,128)} %param.19) | copy-start | bytes 772
  9.4 42.8 %all-to-all-start = ((bf16[16,136,512]{2,1,0:T(8,128)(2,1)}), bf16[16,136,512]{2,1,0:T(8,128)(2,1)S(1)}, u32[]{:S(2)}, u32[]{:S(2)}) async-start(bf16[16,136,512]{2,1,0:T(8,128)(2,1)} %copy-done.6), calls=%async_computation | async-start | bytes 4456448 | tf_op jit(solution)/shard_map/all_to_all | solution.py:463
  23.8 9.0 %copy-start.3 = (bf16[264,2048]{1,0:T(8,128)(2,1)S(1)}, bf16[264,2048]{1,0:T(8,128)(2,1)}, u32[]{:S(2)}) copy-start(bf16[264,2048]{1,0:T(8,128)(2,1)} %pack.1.refs_0_) | copy-start | bytes 3244036
  30.8 22.2 %copy-start.17 = (f32[128]{0:T(128)S(1)}, f32[128]{0:T(128)}, u32[]{:S(2)}) copy-start(f32[128]{0:T(128)} %param.18) | copy-start | bytes 1540
  31.9 14.1 %collective-permute-start.6 = (bf16[136,2048]{1,0:T(8,128)(2,1)S(1)}, bf16[136,2048]{1,0:T(8,128)(2,1)}, u32[]{:S(2)}, u32[]{:S(2)}) collective-permute-start(bf16[136,2048]{1,0:T(8,128)(2,1)S(1)} %slice.53), channel_id=1, source_target_pairs={{0,32},{32,64},{64,96},{96,0},{1,33},{33,65},{65,97},{97,1},{2,34}... | collective-permute-start | bytes 1671176 | tf_op jit(solution)/shard_map/ppermute | solution.py:24
  32.8 18.4 %collective-permute-start = (bf16[264,2048]{1,0:T(8,128)(2,1)S(1)}, bf16[264,2048]{1,0:T(8,128)(2,1)S(1)}, u32[]{:S(2)}, u32[]{:S(2)}) collective-permute-start(bf16[264,2048]{1,0:T(8,128)(2,1)S(1)} %copy-done.3), channel_id=1, source_target_pairs={{0,16},{16,0},{1,17},{17,1},{2,18},{18,2},{3,19},{19,3},{4,20},{20... | collective-permute-start | bytes 3244040 | tf_op jit(solution)/shard_map/ppermute | solution.py:24
  35.0 18.0 %collective-permute-start.3 = (bf16[264,2048]{1,0:T(8,128)(2,1)}, bf16[264,2048]{1,0:T(8,128)(2,1)}, u32[]{:S(2)}, u32[]{:S(2)}) collective-permute-start(bf16[264,2048]{1,0:T(8,128)(2,1)} %collective-permute-done.1.refs_2_), channel_id=1, source_target_pairs={{0,16},{16,0},{1,17},{17,1},{2,18},{18,2},{3,19},{19,3},{4,20},{20... | collective-permute-start | bytes 3244040 | tf_op jit(solution)/shard_map/ppermute | solution.py:24
  35.0 18.0 %collective-permute-start.4 = (bf16[264,2048]{1,0:T(8,128)(2,1)}, bf16[264,2048]{1,0:T(8,128)(2,1)}, u32[]{:S(2)}, u32[]{:S(2)}) collective-permute-start(bf16[264,2048]{1,0:T(8,128)(2,1)} %collective-permute-done.2.refs_4_.refs_0_), channel_id=1, source_target_pairs={{0,16},{16,0},{1,17},{17,1},{2,18},{18,2},{3,19},{19,3},{4,20},{20... | collective-permute-start | bytes 3244040 | tf_op jit(solution)/shard_map/ppermute | solution.py:24
  36.6 13.7 %collective-permute-start.5 = (bf16[128,2048]{1,0:T(8,128)(2,1)S(1)}, bf16[128,2048]{1,0:T(8,128)(2,1)}, u32[]{:S(2)}, u32[]{:S(2)}) collective-permute-start(bf16[128,2048]{1,0:T(8,128)(2,1)S(1)} %slice.52), channel_id=1, source_target_pairs={{0,96},{32,0},{64,32},{96,64},{1,97},{33,1},{65,33},{97,65},{2,98}... | collective-permute-start | bytes 1572872 | tf_op jit(solution)/shard_map/ppermute | solution.py:24
  46.0 6.9 %collective-permute-start.8 = (bf16[136,2048]{1,0:T(8,128)(2,1)}, bf16[136,2048]{1,0:T(8,128)(2,1)}, u32[]{:S(2)}, u32[]{:S(2)}) collective-permute-start(bf16[136,2048]{1,0:T(8,128)(2,1)} %collective-permute-done.6.refs_7_.refs_3_), channel_id=1, source_target_pairs={{0,16},{16,0},{1,17},{17,1},{2,18},{18,2},{3,19},{19,3},{4,20},{20... | collective-permute-start | bytes 1671176 | tf_op jit(solution)/shard_map/ppermute | solution.py:24
  50.3 2.7 %collective-permute-start.7 = (bf16[128,2048]{1,0:T(8,128)(2,1)}, bf16[128,2048]{1,0:T(8,128)(2,1)}, u32[]{:S(2)}, u32[]{:S(2)}) collective-permute-start(bf16[128,2048]{1,0:T(8,128)(2,1)} %collective-permute-done.5.refs_6_.refs_2_), channel_id=1, source_target_pairs={{0,16},{16,0},{1,17},{17,1},{2,18},{18,2},{3,19},{19,3},{4,20},{20... | collective-permute-start | bytes 1572872 | tf_op jit(solution)/shard_map/ppermute | solution.py:24
  51.2 1.0 copy-start.7
  53.0 1.2 copy-start.1
  54.2 1.2 copy-start.4
  55.5 1.2 copy-start.8
  66.8 10.9 %copy-start.16 = (f32[128]{0:T(128)S(1)}, f32[128]{0:T(128)}, u32[]{:S(2)}) copy-start(f32[128]{0:T(128)} %param.17) | copy-start | bytes 1540
  66.8 57.9 %all-to-all-start.1 = ((bf16[128,32,256]{2,1,0:T(8,128)(2,1)}), bf16[128,32,256]{2,1,0:T(8,128)(2,1)}, u32[]{:S(2)}, u32[]{:S(2)}) async-start(bf16[128,32,256]{2,1,0:T(8,128)(2,1)} %get-tuple-element.21), calls=%async_computation.1 | async-start | bytes 4194304 | tf_op jit(solution)/shard_map/all_to_all | solution.py:469
  77.7 1.2 copy-start.2
  79.0 1.0 copy-start.10
  80.0 1.0 copy-start.12
  81.1 12.9 %copy-start.5 = (bf16[264,2048]{1,0:T(8,128)(2,1)S(1)}, bf16[264,2048]{1,0:T(8,128)(2,1)}, u32[]{:S(2)}) copy-start(bf16[264,2048]{1,0:T(8,128)(2,1)} %pack.1.refs_0_) | copy-start | bytes 3244036
  81.1 12.9 %copy-start.9 = (bf16[264,2048]{1,0:T(8,128)(2,1)S(1)}, bf16[264,2048]{1,0:T(8,128)(2,1)}, u32[]{:S(2)}) copy-start(bf16[264,2048]{1,0:T(8,128)(2,1)} %copy-done.7) | copy-start | bytes 3244036
  81.1 12.9 %copy-start.11 = (bf16[2048,128]{1,0:T(8,128)(2,1)S(1)}, bf16[2048,128]{1,0:T(8,128)(2,1)}, u32[]{:S(2)}) copy-start(bf16[2048,128]{1,0:T(8,128)(2,1)} %get-tuple-element.17.refs_8_.refs_10_) | copy-start | bytes 1572868
  90.6 21.9 %collective-permute-start.10 = (bf16[2,2,264,256]{3,2,1,0:T(8,128)(2,1)S(1)}, bf16[2,2,264,256]{3,2,1,0:T(8,128)(2,1)S(1)}, u32[]{:S(2)}, u32[]{:S(2)}) collective-permute-start(bf16[2,2,264,256]{3,2,1,0:T(8,128)(2,1)S(1)} %bitcast.53), channel_id=1, source_target_pairs={{0,96},{32,0},{64,32},{96,64},{1,97},{33,1},{65,33},{97,65},{2,98}... | collective-permute-start | bytes 1622024 | tf_op jit(solution)/shard_map/ppermute | solution.py:24
  102.6 12.7 %collective-permute-start.12 = (bf16[2,264,256]{2,1,0:T(8,128)(2,1)S(1)}, bf16[2,264,256]{2,1,0:T(8,128)(2,1)S(1)}, u32[]{:S(2)}, u32[]{:S(2)}) collective-permute-start(bf16[2,264,256]{2,1,0:T(8,128)(2,1)S(1)} %slice.71), channel_id=1, source_target_pairs={{0,32},{32,64},{64,96},{96,0},{1,33},{33,65},{65,97},{97,1},{2,34}... | collective-permute-start | bytes 811016 | tf_op jit(solution)/shard_map/ppermute | solution.py:24
  102.7 19.5 %collective-permute-start.9 = (bf16[264,256]{1,0:T(8,128)(2,1)S(1)}, bf16[264,256]{1,0:T(8,128)(2,1)S(1)}, u32[]{:S(2)}, u32[]{:S(2)}) collective-permute-start(bf16[264,256]{1,0:T(8,128)(2,1)S(1)} %get-tuple-element.28), channel_id=1, source_target_pairs={{0,16},{16,0},{1,17},{17,1},{2,18},{18,2},{3,19},{19,3},{4,20},{20... | collective-permute-start | bytes 405512 | tf_op jit(solution)/shard_map/ppermute | solution.py:24
  112.5 8.4 %collective-permute-start.14 = (bf16[2,264,256]{2,1,0:T(8,128)(2,1)S(1)}, bf16[2,264,256]{2,1,0:T(8,128)(2,1)S(1)}, u32[]{:S(2)}, u32[]{:S(2)}) collective-permute-start(bf16[2,264,256]{2,1,0:T(8,128)(2,1)S(1)} %slice_bitcast_fusion), channel_id=1, source_target_pairs={{0,96},{32,0},{64,32},{96,64},{1,97},{33,1},{65,33},{97,65},{2,98}... | collective-permute-start | bytes 811016 | tf_op jit(solution)/shard_map/ppermute | solution.py:24
  115.3 6.8 %collective-permute-start.13 = (bf16[264,256]{1,0:T(8,128)(2,1)S(1)}, bf16[264,256]{1,0:T(8,128)(2,1)S(1)}, u32[]{:S(2)}, u32[]{:S(2)}) collective-permute-start(bf16[264,256]{1,0:T(8,128)(2,1)S(1)} %get-tuple-element.32), channel_id=1, source_target_pairs={{0,16},{16,0},{1,17},{17,1},{2,18},{18,2},{3,19},{19,3},{4,20},{20... | collective-permute-start | bytes 405512 | tf_op jit(solution)/shard_map/ppermute | solution.py:24
  116.1 6.1 %collective-permute-start.11 = (bf16[264,256]{1,0:T(8,128)(2,1)S(1)}, bf16[264,256]{1,0:T(8,128)(2,1)S(1)}, u32[]{:S(2)}, u32[]{:S(2)}) collective-permute-start(bf16[264,256]{1,0:T(8,128)(2,1)S(1)} %get-tuple-element.26), channel_id=1, source_target_pairs={{0,16},{16,0},{1,17},{17,1},{2,18},{18,2},{3,19},{19,3},{4,20},{20... | collective-permute-start | bytes 405512 | tf_op jit(solution)/shard_map/ppermute | solution.py:24
  120.9 2.2 %collective-permute-start.15 = (bf16[264,256]{1,0:T(8,128)(2,1)S(1)}, bf16[264,256]{1,0:T(8,128)(2,1)S(1)}, u32[]{:S(2)}, u32[]{:S(2)}) collective-permute-start(bf16[264,256]{1,0:T(8,128)(2,1)S(1)} %get-tuple-element.30), channel_id=1, source_target_pairs={{0,16},{16,0},{1,17},{17,1},{2,18},{18,2},{3,19},{19,3},{4,20},{20... | collective-permute-start | bytes 405512 | tf_op jit(solution)/shard_map/ppermute | solution.py:24

commit v3 on v2

--- a/solution.py
+++ b/solution.py
@@ -144,34 +144,53 @@
 
     def kernel(ys, piece, core_ref, *refs):
         w_ref, gain_ref, cos_ref, sin_ref, k_hbm, v_hbm, b_hbm = refs[count : count + 7]
-        w_kv, kv, k_out, v_out, b_out, sems = refs[count + 7 :]
+        w_kv, kv, k_out, v_out, b_out, sems, xs, takes = refs[count + 7 :]
         step = pl.program_id(0)
 
         def send(i):
             at = pl.multiple_of(ys[i] * 8, 8)
             return pltpu.make_async_copy(b_out.at[i], b_hbm.at[:, pl.ds(at, 8), :], sems.at[i])
 
+        def fetch(i):
+            first = sum(len(p) for p in pairs[:i])
+            moves = []
+            row, side = 0, 0
+            for n in range(first, first + len(pairs[i])):
+                height = refs[n].shape[0]
+                to = xs.at[2 * i + side, pl.ds(row, height)]
+                moves.append(pltpu.make_async_copy(refs[n], to, takes.at[n]))
+                row += height
+                if row == TOK + ROUTE:
+                    row, side = 0, side + 1
+            return moves
+
         @pl.when(step == 0)
         def _():
+            for i in range(len(pairs)):
+                for move in fetch(i):
+                    move.start()
             take_weights(w_ref, slice(2 * HEAD, 4 * HEAD), w_kv)
 
-        def go(part):
-            at = 0
+        def arrive(i):
+            for move in fetch(i):
+                move.wait()
+
+        for i in range(len(pairs)):
+            pl.when(step == i)(lambda i=i: arrive(i))
+
+        def go():
             codes = []
-            for ref in part:
-                rows = data_rows(ref)
-                raw = jnp.dot(ref[0:rows, :], w_kv[...], preferred_element_type=jnp.float32)
-                put = slice(at, at + rows)
+            for side in range(2):
+                x = 2 * step + side
+                raw = jnp.dot(xs[x, 0:TOK, :], w_kv[...], preferred_element_type=jnp.float32)
+                put = slice(side * TOK, (side + 1) * TOK)
                 kv[put, :HEAD] = norm_rope(
                     raw[:, :HEAD], gain_ref[...], cos_ref[0, put, :], sin_ref[0, put, :]
                 )
                 kv[put, HEAD:] = raw[:, HEAD:].astype(jnp.bfloat16)
-                if rows < ref.shape[0]:
-                    lead = ref[rows:, 0:TOK].astype(jnp.float32)
-                    side = len(codes)
-                    mine = core_ref[0] + side - 2 * core_ref[0] * side
-                    codes.append((lead[0:1] * 8 + lead[1:2]).astype(jnp.int32) + mine * MOST)
-                at += rows
+                lead = xs[x, TOK:, 0:TOK].astype(jnp.float32)
+                mine = core_ref[0] + side - 2 * core_ref[0] * side
+                codes.append((lead[0:1] * 8 + lead[1:2]).astype(jnp.int32) + mine * MOST)
             place = lax.broadcasted_iota(jnp.int32, (8 * 128, 2 * TOK), 0)
             pick = (place == jnp.concatenate(codes, axis=1)).astype(jnp.bfloat16)
             got = jnp.dot(pick, kv[...], preferred_element_type=jnp.float32)
@@ -182,10 +201,7 @@
                 k_out[to, :] = kv[side * TOK : (side + 1) * TOK, :HEAD]
                 v_out[to, :] = kv[side * TOK : (side + 1) * TOK, HEAD:]
 
-        at = 0
-        for i, p in enumerate(pairs):
-            pl.when(step == i)(lambda part=refs[at : at + len(p)]: go(part))
-            at += len(p)
+        go()
 
         @pl.when(step == 3)
         def _():
@@ -209,9 +225,9 @@
             pltpu.HBM((8 * TOK, HEAD), jnp.bfloat16),
             pltpu.HBM((128, 32, 2 * HEAD), jnp.bfloat16),
         ],
-        [WHOLE] * (count + 2) + [table] * 2,
+        [FAR] * count + [WHOLE] * 2 + [table] * 2,
         [FAR] * 3,
-        14,
+        26,
         (2 * 2048 * 2048 * 256, 12),
         "keys",
         [
@@ -221,6 +237,8 @@
             pltpu.VMEM((8 * TOK, HEAD), jnp.bfloat16),
             pltpu.VMEM((4, 128, 8, 2 * HEAD), jnp.bfloat16),
             pltpu.SemaphoreType.DMA((6,)),
+            pltpu.VMEM((8, TOK + ROUTE, 2048), jnp.bfloat16),
+            pltpu.SemaphoreType.DMA((count,)),
         ],
         (4,),
         maps,

time: 131 us -> 129 us (0.985)
  waiting for transfers between devices: 32.6 us -> 30.8 us
    pallas_call x1, Pallas kernels: 10.1 us -> 7.77 us  [keys(): call(kernel, [pltpu.HBM((8 * TOK, HEAD), jnp.bfloat16), pltpu.HBM((8 * TO...]
    ppermute x16, waiting for transfers between devices: 32.6 us -> 30.8 us  [shift(): lax.ppermute(value, axis, [(i, (i + by) % size) for i in range(size)])]
    pallas_call x2, Pallas kernels: 18 us -> 19.4 us  [attend(): call(kernel, shape(n, TOK + ROUTE, 2 * HEAD), [WHOLE] * (count + 2) + [ta...]
  transfers between devices with their start and end apart: 18 -> 18, of which waited for: 7 -> 7; matrix products, arithmetic and copies ran while one was open for 8% -> 8% of each run, Pallas kernels for 15% -> 17%
where the time goes in v3:
time: 129 us; the launch traced here: 128 us
  starting transfers between devices  39.6 us (31%)
  Pallas kernels  37.4 us (29%)
  waiting for transfers between devices  30.8 us (24%)
  local copies, waits for them, and re-layouts  12.7 us (10%)
  other arithmetic  6.57 us (5%)
    ppermute x16, waiting for transfers between devices, shift(): lax.ppermute(value, axis, [(i, (i + by) % size) for i in range(size)])  30.8 us
    ppermute x16, starting transfers between devices, shift(): lax.ppermute(value, axis, [(i, (i + by) % size) for i in range(size)])  21.3 us
    pallas_call x2, Pallas kernels, attend(): call(kernel, shape(n, TOK + ROUTE, 2 * HEAD), [WHOLE] * (count + 2) + [ta...  19.4 us
    all_to_all x1, starting transfers between devices, shards(): lax.all_to_all(buckets, CTX + FSDP, split_axis=0, concat_axis=0, tiled=True)  10.6 us
    unnamed x50, local copies, waits for them, and re-layouts  9.61 us
    pallas_call x1, Pallas kernels, keys(): call(kernel, [pltpu.HBM((8 * TOK, HEAD), jnp.bfloat16), pltpu.HBM((8 * TO...  7.77 us
    all_to_all x1, starting transfers between devices, shards(): w = lax.all_to_all(w, FSDP, split_axis=0, concat_axis=0, tiled=True)  7.73 us
    pallas_call x1, Pallas kernels, fill_cache(): call(cache_kernel, shape(512, 2048), [WHOLE, FAR], WHOLE, 10, (2 * 512 *...  5.73 us
  transfers between devices with their start and end apart: 18, of which 7 were waited for; matrix products, arithmetic and copies ran while one was open for 8% of the time, Pallas kernels for 17%

profile of v3, /device:TPU:1, one launch (start us, length us, event | category | flops | bytes accessed | tf_op | source)
XLA Modules:
  0.0 128.4 jit_solution(13472213860748011040)
XLA Ops:
  0.7 2.7 %pack.1.refs_0_ = bf16[264,2048]{1,0:T(8,128)(2,1)} custom-call(bf16[256,2048]{1,0:T(8,128)(2,1)} %bitcast.61, s32[1,256]{1,0:T(1,128)} %bitcast.66, f32[1,2048]{1,0:T(1,128)} %bitcast.69), custom_call_target="tpu_custom_call" | custom-call | bytes 2097152 | tf_op jit(solution)/shard_map/pack/pallas_call | solution.py:86
  3.4 2.2 %collective-permute-start.2 = (bf16[264,2048]{1,0:T(8,128)(2,1)}, bf16[264,2048]{1,0:T(8,128)(2,1)}, u32[]{:S(2)}, u32[]{:S(2)}) collective-permute-start(bf16[264,2048]{1,0:T(8,128)(2,1)} %pack.1.refs_0_), channel_id=1, source_target_pairs={{0,32},{32,64},{64,96},{96,0},{1,33},{33,65},{65,97},{97,1},{2,34}... | collective-permute-start | bytes 3244040 | tf_op jit(solution)/shard_map/ppermute | solution.py:24
  5.6 1.5 %collective-permute-start.1 = (bf16[264,2048]{1,0:T(8,128)(2,1)}, bf16[264,2048]{1,0:T(8,128)(2,1)}, u32[]{:S(2)}, u32[]{:S(2)}) collective-permute-start(bf16[264,2048]{1,0:T(8,128)(2,1)} %pack.1.refs_0_), channel_id=1, source_target_pairs={{0,96},{32,0},{64,32},{96,64},{1,97},{33,1},{65,33},{97,65},{2,98}... | collective-permute-start | bytes 3244040 | tf_op jit(solution)/shard_map/ppermute | solution.py:24
  7.2 0.2 convert_reduce_fusion
  7.4 0.2 select_reduce_fusion
  7.8 0.2 spread_weights.1
  8.0 1.4 %copy-done.6 = bf16[16,136,512]{2,1,0:T(8,128)(2,1)} copy-done((bf16[16,136,512]{2,1,0:T(8,128)(2,1)}, bf16[16,136,512]{2,1,0:T(8,128)(2,1)S(1)}, u32[]{:S(2)}) %copy-start.6) | copy-done | bytes 2228248
  9.4 7.7 %all-to-all-start = ((bf16[16,136,512]{2,1,0:T(8,128)(2,1)}), bf16[16,136,512]{2,1,0:T(8,128)(2,1)S(1)}, u32[]{:S(2)}, u32[]{:S(2)}) async-start(bf16[16,136,512]{2,1,0:T(8,128)(2,1)} %copy-done.6), calls=%async_computation | async-start | bytes 4456448 | tf_op jit(solution)/shard_map/all_to_all | solution.py:481
  17.4 0.2 dynamic-slice_reduce_fusion
  17.6 0.2 select_reduce_fusion.2.piece
  18.1 0.2 reduce-window.4
  18.4 0.1 select_reduce_fusion.1
  18.5 3.7 %fusion = (f32[4,512,64]{2,1,0:T(8,128)S(1)}, f32[4,512,64]{2,1,0:T(8,128)S(1)}, f32[4,512,64]{2,1,0:T(8,128)S(1)}) fusion(f32[64]{0:T(128)S(1)} %multiply_exponential_fusion, f32[4,512]{1,0:T(4,128)S(1)} %subtract_convert_fusion), kind=kLoop, calls=%fused_computation.6 | loop fusion | flops 262144 | bytes 1581312 | tf_op jit(solution)/shard_map/neg | solution.py:455
  22.2 1.6 %pad_maximum_fusion = (f32[4,512,128]{2,1,0:T(8,128)S(1)}, f32[4,512,128]{2,1,0:T(8,128)}) fusion(f32[4,512,64]{2,1,0:T(8,128)S(1)} %get-tuple-element.36, f32[4,512,64]{2,1,0:T(8,128)S(1)} %get-tuple-element.35, f32[4,512,64]{2,1,0:T(8,128)S(1)} %get-tuple-element.34), kind=kLoop, calls=%fused_computation.2 | loop fusion | flops 524288 | bytes 3670016 | tf_op jit(solution)/shard_map/concatenate | solution.py:454
  23.8 7.0 %collective-permute-done.2.refs_4_.refs_0_ = bf16[264,2048]{1,0:T(8,128)(2,1)} collective-permute-done((bf16[264,2048]{1,0:T(8,128)(2,1)}, bf16[264,2048]{1,0:T(8,128)(2,1)}, u32[]{:S(2)}, u32[]{:S(2)}) %collective-permute-start.2) | collective-permute-done | bytes 1081376 | tf_op jit(solution)/shard_map/ppermute | solution.py:24
  30.8 1.1 slice.53
  31.9 0.9 collective-permute-start.6
  32.8 2.1 %collective-permute-start = (bf16[264,2048]{1,0:T(8,128)(2,1)S(1)}, bf16[264,2048]{1,0:T(8,128)(2,1)S(1)}, u32[]{:S(2)}, u32[]{:S(2)}) collective-permute-start(bf16[264,2048]{1,0:T(8,128)(2,1)S(1)} %copy-done.3), channel_id=1, source_target_pairs={{0,16},{16,0},{1,17},{17,1},{2,18},{18,2},{3,19},{19,3},{4,20},{20... | collective-permute-start | bytes 3244040 | tf_op jit(solution)/shard_map/ppermute | solution.py:24
  35.0 0.5 collective-permute-start.4
  35.5 1.1 slice.52
  36.6 1.4 %collective-permute-start.5 = (bf16[128,2048]{1,0:T(8,128)(2,1)S(1)}, bf16[128,2048]{1,0:T(8,128)(2,1)}, u32[]{:S(2)}, u32[]{:S(2)}) collective-permute-start(bf16[128,2048]{1,0:T(8,128)(2,1)S(1)} %slice.52), channel_id=1, source_target_pairs={{0,96},{32,0},{64,32},{96,64},{1,97},{33,1},{65,33},{97,65},{2,98}... | collective-permute-start | bytes 1572872 | tf_op jit(solution)/shard_map/ppermute | solution.py:24
  38.0 8.0 %collective-permute-done.6.refs_7_.refs_3_ = bf16[136,2048]{1,0:T(8,128)(2,1)} collective-permute-done((bf16[136,2048]{1,0:T(8,128)(2,1)S(1)}, bf16[136,2048]{1,0:T(8,128)(2,1)}, u32[]{:S(2)}, u32[]{:S(2)}) %collective-permute-start.6) | collective-permute-done | bytes 557088 | tf_op jit(solution)/shard_map/ppermute | solution.py:24
  46.0 2.3 %collective-permute-start.8 = (bf16[136,2048]{1,0:T(8,128)(2,1)}, bf16[136,2048]{1,0:T(8,128)(2,1)}, u32[]{:S(2)}, u32[]{:S(2)}) collective-permute-start(bf16[136,2048]{1,0:T(8,128)(2,1)} %collective-permute-done.6.refs_7_.refs_3_), channel_id=1, source_target_pairs={{0,16},{16,0},{1,17},{17,1},{2,18},{18,2},{3,19},{19,3},{4,20},{20... | collective-permute-start | bytes 1671176 | tf_op jit(solution)/shard_map/ppermute | solution.py:24
  48.4 1.9 %collective-permute-done.5.refs_6_.refs_2_ = bf16[128,2048]{1,0:T(8,128)(2,1)} collective-permute-done((bf16[128,2048]{1,0:T(8,128)(2,1)S(1)}, bf16[128,2048]{1,0:T(8,128)(2,1)}, u32[]{:S(2)}, u32[]{:S(2)}) %collective-permute-start.5) | collective-permute-done | bytes 524320 | tf_op jit(solution)/shard_map/ppermute | solution.py:24
  50.3 0.8 collective-permute-start.7
  51.2 1.0 copy-done.7
  52.2 0.8 collective-permute-done.7.refs_8_.refs_4_
  53.0 1.2 copy-done.1
  54.2 1.2 copy-done.4
  55.5 1.2 copy-done.8
  56.7 7.8 %keys.1 = (bf16[2048,128]{1,0:T(8,128)(2,1)}, bf16[2048,128]{1,0:T(8,128)(2,1)}, bf16[128,32,256]{2,1,0:T(8,128)(2,1)}) custom-call(s32[4]{0:T(128)S(1)} %get-tuple-element.25.ys, s32[8]{0:T(128)S(1)} %select_reduce_fusion.2.piece, s32[1]{0:T(128)} %bitcast.core_ref, bf16[264,2048]{1,0:T(8,128)(2,1)S(1)} %copy-done.4, bf16[264,2048]{1,0:T(8,128)(2,1)S(1)} %copy-done.8, ...), custom_call_target="tpu_custom_call" | custom-call | flops 2147483648 | bytes 12582912 | tf_op jit(solution)/shard_map/keys/pallas_call | solution.py:221
  64.5 10.6 %all-to-all-start.1 = ((bf16[128,32,256]{2,1,0:T(8,128)(2,1)}), bf16[128,32,256]{2,1,0:T(8,128)(2,1)}, u32[]{:S(2)}, u32[]{:S(2)}) async-start(bf16[128,32,256]{2,1,0:T(8,128)(2,1)} %get-tuple-element.21), calls=%async_computation.1 | async-start | bytes 4194304 | tf_op jit(solution)/shard_map/all_to_all | solution.py:487
  75.2 0.1 copy.22
  75.4 1.2 copy-done.2
  76.6 1.0 copy-done.10
  77.7 1.0 copy-done.12
  78.7 10.0 %attend.3 = bf16[4,264,256]{2,1,0:T(8,128)(2,1)S(1)} custom-call(s32[8]{0:T(128)S(1)} %select_reduce_fusion.2.piece, s32[8]{0:T(128)S(1)} %add.153.ctx.ctx_of, s32[8]{0:T(128)S(1)} %and_select_fusion.4.lows, s32[4]{0:T(128)S(1)} %bitcast_subtract_fusion.begins, bf16[264,2048]{1,0:T(8,128)(2,1)} %collective-permute-done.2.refs_4_.refs_0_, ...), custom_call_target="tpu_custom_call" | custom-call | flops 2147483648 | bytes 4194304 | tf_op jit(solution)/shard_map/attend/pallas_call | solution.py:327
  88.7 3.9 %collective-permute-start.10 = (bf16[2,2,264,256]{3,2,1,0:T(8,128)(2,1)S(1)}, bf16[2,2,264,256]{3,2,1,0:T(8,128)(2,1)S(1)}, u32[]{:S(2)}, u32[]{:S(2)}) collective-permute-start(bf16[2,2,264,256]{3,2,1,0:T(8,128)(2,1)S(1)} %bitcast.53), channel_id=1, source_target_pairs={{0,96},{32,0},{64,32},{96,64},{1,97},{33,1},{65,33},{97,65},{2,98}... | collective-permute-start | bytes 1622024 | tf_op jit(solution)/shard_map/ppermute | solution.py:24
  92.7 9.4 %attend.2 = bf16[4,264,256]{2,1,0:T(8,128)(2,1)S(1)} custom-call(s32[8]{0:T(128)S(1)} %select_reduce_fusion.2.piece, s32[8]{0:T(128)S(1)} %add.153.ctx.ctx_of, s32[8]{0:T(128)S(1)} %and_select_fusion.4.lows, s32[4]{0:T(128)S(1)} %bitcast_subtract_fusion.begins, bf16[264,2048]{1,0:T(8,128)(2,1)S(1)} %copy-done.5, bf16[264,2048]{1,0:T(8,128)(2,1)S(1)} %copy-done.9, ...), custom_call_target="tpu_custom_call" | custom-call | flops 2147483648 | bytes 4194304 | tf_op jit(solution)/shard_map/attend/pallas_call | solution.py:327
  102.2 0.7 collective-permute-start.9
  102.9 7.2 %collective-permute-done.10 = bf16[2,2,264,256]{3,2,1,0:T(8,128)(2,1)S(1)} collective-permute-done((bf16[2,2,264,256]{3,2,1,0:T(8,128)(2,1)S(1)}, bf16[2,2,264,256]{3,2,1,0:T(8,128)(2,1)S(1)}, u32[]{:S(2)}, u32[]{:S(2)}) %collective-permute-start.10) | collective-permute-done | bytes 540704 | tf_op jit(solution)/shard_map/ppermute | solution.py:24
  110.2 2.7 %collective-permute-start.14 = (bf16[2,264,256]{2,1,0:T(8,128)(2,1)S(1)}, bf16[2,264,256]{2,1,0:T(8,128)(2,1)S(1)}, u32[]{:S(2)}, u32[]{:S(2)}) collective-permute-start(bf16[2,264,256]{2,1,0:T(8,128)(2,1)S(1)} %slice_bitcast_fusion), channel_id=1, source_target_pairs={{0,96},{32,0},{64,32},{96,64},{1,97},{33,1},{65,33},{97,65},{2,98}... | collective-permute-start | bytes 811016 | tf_op jit(solution)/shard_map/ppermute | solution.py:24
  112.9 0.8 collective-permute-start.13
  113.8 4.9 %collective-permute-done.14 = bf16[2,264,256]{2,1,0:T(8,128)(2,1)S(1)} collective-permute-done((bf16[2,264,256]{2,1,0:T(8,128)(2,1)S(1)}, bf16[2,264,256]{2,1,0:T(8,128)(2,1)S(1)}, u32[]{:S(2)}, u32[]{:S(2)}) %collective-permute-start.14) | collective-permute-done | bytes 270368 | tf_op jit(solution)/shard_map/ppermute | solution.py:24
  118.7 1.1 collective-permute-start.15
  119.9 1.0 collective-permute-done.15
  120.8 1.6 %spread.1 = (bf16[256,2048]{1,0:T(8,128)(2,1)}, bf16[8,8,128]{2,1,0:T(8,128)(2,1)S(1)}) custom-call(s32[8]{0:T(128)S(1)} %add.153.ctx.ctx_of, bf16[1,264,256]{2,1,0:T(8,128)(2,1)S(1)} %get-tuple-element.29.refs_0_, bf16[1,264,256]{2,1,0:T(8,128)(2,1)S(1)} %bitcast.54, bf16[1,264,256]{2,1,0:T(8,128)(2,1)S(1)} %get-tuple-element.27.refs_2_, ...), custom_call_target="tpu_custom_call" | custom-call | bytes 2097152 | tf_op jit(solution)/shard_map/spread/pallas_call | solution.py:410
  122.5 5.7 %fill_cache.1 = bf16[512,2048]{1,0:T(8,128)(2,1)} custom-call(bf16[8,8,128]{2,1,0:T(8,128)(2,1)S(1)} %get-tuple-element.20.leads, bf16[8,512,256]{2,1,0:T(8,128)(2,1)} %bitcast.29.got), custom_call_target="tpu_custom_call" | custom-call | flops 1073741824 | bytes 4194304 | tf_op jit(solution)/shard_map/fill_cache/pallas_call | solution.py:385
  (88 shorter events, 1.6 us)
Async XLA Ops:
  0.6 16.7 %copy-start = (s32[16,8]{0,1:T(8,128)S(1)}, s32[16,8]{0,1:T(8,128)}, u32[]{:S(2)}) copy-start(s32[16,8]{0,1:T(8,128)} %param.20) | copy-start | bytes 1540
  0.6 6.5 %copy-start.18 = (s32[1,1,256]{2,1,0:T(1,128)S(1)}, s32[1,1,256]{2,1,0:T(1,128)}, u32[]{:S(2)}) copy-start(s32[1,1,256]{2,1,0:T(1,128)} %param.21) | copy-start | bytes 3076
  0.7 6.5 %copy-start.20 = (s32[1,1,256]{2,1,0:T(1,128)S(1)}, s32[1,1,256]{2,1,0:T(1,128)}, u32[]{:S(2)}) copy-start(s32[1,1,256]{2,1,0:T(1,128)} %param.22) | copy-start | bytes 3076
  0.7 7.1 %copy-start.13 = (bf16[128,256]{1,0:T(8,128)(2,1)S(1)}, bf16[128,256]{1,0:T(8,128)(2,1)}, u32[]{:S(2)}) copy-start(bf16[128,256]{1,0:T(8,128)(2,1)} %a.1) | copy-start | bytes 196612
  0.7 7.1 %copy-start.14 = (bf16[128,128]{1,0:T(8,128)(2,1)S(1)}, bf16[128,128]{1,0:T(8,128)(2,1)}, u32[]{:S(2)}) copy-start(bf16[128,128]{1,0:T(8,128)(2,1)} %b.1) | copy-start | bytes 98308
  0.7 7.1 %copy-start.15 = (bf16[128,128]{1,0:T(8,128)(2,1)S(1)}, bf16[128,128]{1,0:T(8,128)(2,1)}, u32[]{:S(2)}) copy-start(bf16[128,128]{1,0:T(8,128)(2,1)} %c.1) | copy-start | bytes 98308
  3.4 27.4 %collective-permute-start.2 = (bf16[264,2048]{1,0:T(8,128)(2,1)}, bf16[264,2048]{1,0:T(8,128)(2,1)}, u32[]{:S(2)}, u32[]{:S(2)}) collective-permute-start(bf16[264,2048]{1,0:T(8,128)(2,1)} %pack.1.refs_0_), channel_id=1, source_target_pairs={{0,32},{32,64},{64,96},{96,0},{1,33},{33,65},{65,97},{97,1},{2,34}... | collective-permute-start | bytes 3244040 | tf_op jit(solution)/shard_map/ppermute | solution.py:24
  5.6 25.2 %collective-permute-start.1 = (bf16[264,2048]{1,0:T(8,128)(2,1)}, bf16[264,2048]{1,0:T(8,128)(2,1)}, u32[]{:S(2)}, u32[]{:S(2)}) collective-permute-start(bf16[264,2048]{1,0:T(8,128)(2,1)} %pack.1.refs_0_), channel_id=1, source_target_pairs={{0,96},{32,0},{64,32},{96,64},{1,97},{33,1},{65,33},{97,65},{2,98}... | collective-permute-start | bytes 3244040 | tf_op jit(solution)/shard_map/ppermute | solution.py:24
  8.0 1.4 %copy-start.6 = (bf16[16,136,512]{2,1,0:T(8,128)(2,1)}, bf16[16,136,512]{2,1,0:T(8,128)(2,1)S(1)}, u32[]{:S(2)}) copy-start(bf16[16,136,512]{2,1,0:T(8,128)(2,1)S(1)} %spread_weights.1) | copy-start | bytes 6684676
  9.4 7.8 %copy-start.21 = (s32[4]{0:T(128)S(1)}, s32[4]{0:T(128)}, u32[]{:S(2)}) copy-start(s32[4]{0:T(128)} %constant.118.clone) | copy-start | bytes 52
  9.4 8.5 %copy-start.19 = (s32[16,4]{0,1:T(4,128)S(1)}, s32[16,4]{0,1:T(4,128)}, u32[]{:S(2)}) copy-start(s32[16,4]{0,1:T(4,128)} %param.19) | copy-start | bytes 772
  9.4 42.8 %all-to-all-start = ((bf16[16,136,512]{2,1,0:T(8,128)(2,1)}), bf16[16,136,512]{2,1,0:T(8,128)(2,1)S(1)}, u32[]{:S(2)}, u32[]{:S(2)}) async-start(bf16[16,136,512]{2,1,0:T(8,128)(2,1)} %copy-done.6), calls=%async_computation | async-start | bytes 4456448 | tf_op jit(solution)/shard_map/all_to_all | solution.py:481
  23.8 9.0 %copy-start.3 = (bf16[264,2048]{1,0:T(8,128)(2,1)S(1)}, bf16[264,2048]{1,0:T(8,128)(2,1)}, u32[]{:S(2)}) copy-start(bf16[264,2048]{1,0:T(8,128)(2,1)} %pack.1.refs_0_) | copy-start | bytes 3244036
  30.8 22.2 %copy-start.17 = (f32[128]{0:T(128)S(1)}, f32[128]{0:T(128)}, u32[]{:S(2)}) copy-start(f32[128]{0:T(128)} %param.18) | copy-start | bytes 1540
  31.9 14.1 %collective-permute-start.6 = (bf16[136,2048]{1,0:T(8,128)(2,1)S(1)}, bf16[136,2048]{1,0:T(8,128)(2,1)}, u32[]{:S(2)}, u32[]{:S(2)}) collective-permute-start(bf16[136,2048]{1,0:T(8,128)(2,1)S(1)} %slice.53), channel_id=1, source_target_pairs={{0,32},{32,64},{64,96},{96,0},{1,33},{33,65},{65,97},{97,1},{2,34}... | collective-permute-start | bytes 1671176 | tf_op jit(solution)/shard_map/ppermute | solution.py:24
  32.8 18.4 %collective-permute-start = (bf16[264,2048]{1,0:T(8,128)(2,1)S(1)}, bf16[264,2048]{1,0:T(8,128)(2,1)S(1)}, u32[]{:S(2)}, u32[]{:S(2)}) collective-permute-start(bf16[264,2048]{1,0:T(8,128)(2,1)S(1)} %copy-done.3), channel_id=1, source_target_pairs={{0,16},{16,0},{1,17},{17,1},{2,18},{18,2},{3,19},{19,3},{4,20},{20... | collective-permute-start | bytes 3244040 | tf_op jit(solution)/shard_map/ppermute | solution.py:24
  35.0 18.0 %collective-permute-start.3 = (bf16[264,2048]{1,0:T(8,128)(2,1)}, bf16[264,2048]{1,0:T(8,128)(2,1)}, u32[]{:S(2)}, u32[]{:S(2)}) collective-permute-start(bf16[264,2048]{1,0:T(8,128)(2,1)} %collective-permute-done.1.refs_2_), channel_id=1, source_target_pairs={{0,16},{16,0},{1,17},{17,1},{2,18},{18,2},{3,19},{19,3},{4,20},{20... | collective-permute-start | bytes 3244040 | tf_op jit(solution)/shard_map/ppermute | solution.py:24
  35.0 18.0 %collective-permute-start.4 = (bf16[264,2048]{1,0:T(8,128)(2,1)}, bf16[264,2048]{1,0:T(8,128)(2,1)}, u32[]{:S(2)}, u32[]{:S(2)}) collective-permute-start(bf16[264,2048]{1,0:T(8,128)(2,1)} %collective-permute-done.2.refs_4_.refs_0_), channel_id=1, source_target_pairs={{0,16},{16,0},{1,17},{17,1},{2,18},{18,2},{3,19},{19,3},{4,20},{20... | collective-permute-start | bytes 3244040 | tf_op jit(solution)/shard_map/ppermute | solution.py:24
  36.6 13.7 %collective-permute-start.5 = (bf16[128,2048]{1,0:T(8,128)(2,1)S(1)}, bf16[128,2048]{1,0:T(8,128)(2,1)}, u32[]{:S(2)}, u32[]{:S(2)}) collective-permute-start(bf16[128,2048]{1,0:T(8,128)(2,1)S(1)} %slice.52), channel_id=1, source_target_pairs={{0,96},{32,0},{64,32},{96,64},{1,97},{33,1},{65,33},{97,65},{2,98}... | collective-permute-start | bytes 1572872 | tf_op jit(solution)/shard_map/ppermute | solution.py:24
  46.0 6.9 %collective-permute-start.8 = (bf16[136,2048]{1,0:T(8,128)(2,1)}, bf16[136,2048]{1,0:T(8,128)(2,1)}, u32[]{:S(2)}, u32[]{:S(2)}) collective-permute-start(bf16[136,2048]{1,0:T(8,128)(2,1)} %collective-permute-done.6.refs_7_.refs_3_), channel_id=1, source_target_pairs={{0,16},{16,0},{1,17},{17,1},{2,18},{18,2},{3,19},{19,3},{4,20},{20... | collective-permute-start | bytes 1671176 | tf_op jit(solution)/shard_map/ppermute | solution.py:24
  50.3 2.7 %collective-permute-start.7 = (bf16[128,2048]{1,0:T(8,128)(2,1)}, bf16[128,2048]{1,0:T(8,128)(2,1)}, u32[]{:S(2)}, u32[]{:S(2)}) collective-permute-start(bf16[128,2048]{1,0:T(8,128)(2,1)} %collective-permute-done.5.refs_6_.refs_2_), channel_id=1, source_target_pairs={{0,16},{16,0},{1,17},{17,1},{2,18},{18,2},{3,19},{19,3},{4,20},{20... | collective-permute-start | bytes 1572872 | tf_op jit(solution)/shard_map/ppermute | solution.py:24
  51.2 1.0 copy-start.7
  53.0 1.2 copy-start.1
  54.2 1.2 copy-start.4
  55.5 1.2 copy-start.8
  64.5 10.9 %copy-start.16 = (f32[128]{0:T(128)S(1)}, f32[128]{0:T(128)}, u32[]{:S(2)}) copy-start(f32[128]{0:T(128)} %param.17) | copy-start | bytes 1540
  64.5 58.0 %all-to-all-start.1 = ((bf16[128,32,256]{2,1,0:T(8,128)(2,1)}), bf16[128,32,256]{2,1,0:T(8,128)(2,1)}, u32[]{:S(2)}, u32[]{:S(2)}) async-start(bf16[128,32,256]{2,1,0:T(8,128)(2,1)} %get-tuple-element.21), calls=%async_computation.1 | async-start | bytes 4194304 | tf_op jit(solution)/shard_map/all_to_all | solution.py:487
  75.4 1.2 copy-start.2
  76.6 1.0 copy-start.10
  77.7 1.0 copy-start.12
  78.7 13.9 %copy-start.5 = (bf16[264,2048]{1,0:T(8,128)(2,1)S(1)}, bf16[264,2048]{1,0:T(8,128)(2,1)}, u32[]{:S(2)}) copy-start(bf16[264,2048]{1,0:T(8,128)(2,1)} %pack.1.refs_0_) | copy-start | bytes 3244036
  78.7 13.9 %copy-start.9 = (bf16[264,2048]{1,0:T(8,128)(2,1)S(1)}, bf16[264,2048]{1,0:T(8,128)(2,1)}, u32[]{:S(2)}) copy-start(bf16[264,2048]{1,0:T(8,128)(2,1)} %copy-done.7) | copy-start | bytes 3244036
  78.7 13.9 %copy-start.11 = (bf16[2048,128]{1,0:T(8,128)(2,1)S(1)}, bf16[2048,128]{1,0:T(8,128)(2,1)}, u32[]{:S(2)}) copy-start(bf16[2048,128]{1,0:T(8,128)(2,1)} %get-tuple-element.17.refs_8_.refs_10_) | copy-start | bytes 1572868
  88.7 21.4 %collective-permute-start.10 = (bf16[2,2,264,256]{3,2,1,0:T(8,128)(2,1)S(1)}, bf16[2,2,264,256]{3,2,1,0:T(8,128)(2,1)S(1)}, u32[]{:S(2)}, u32[]{:S(2)}) collective-permute-start(bf16[2,2,264,256]{3,2,1,0:T(8,128)(2,1)S(1)} %bitcast.53), channel_id=1, source_target_pairs={{0,96},{32,0},{64,32},{96,64},{1,97},{33,1},{65,33},{97,65},{2,98}... | collective-permute-start | bytes 1622024 | tf_op jit(solution)/shard_map/ppermute | solution.py:24
  102.1 10.8 %collective-permute-start.12 = (bf16[2,264,256]{2,1,0:T(8,128)(2,1)S(1)}, bf16[2,264,256]{2,1,0:T(8,128)(2,1)S(1)}, u32[]{:S(2)}, u32[]{:S(2)}) collective-permute-start(bf16[2,264,256]{2,1,0:T(8,128)(2,1)S(1)} %slice.71), channel_id=1, source_target_pairs={{0,32},{32,64},{64,96},{96,0},{1,33},{33,65},{65,97},{97,1},{2,34}... | collective-permute-start | bytes 811016 | tf_op jit(solution)/shard_map/ppermute | solution.py:24
  102.2 17.6 %collective-permute-start.9 = (bf16[264,256]{1,0:T(8,128)(2,1)S(1)}, bf16[264,256]{1,0:T(8,128)(2,1)S(1)}, u32[]{:S(2)}, u32[]{:S(2)}) collective-permute-start(bf16[264,256]{1,0:T(8,128)(2,1)S(1)} %get-tuple-element.28), channel_id=1, source_target_pairs={{0,16},{16,0},{1,17},{17,1},{2,18},{18,2},{3,19},{19,3},{4,20},{20... | collective-permute-start | bytes 405512 | tf_op jit(solution)/shard_map/ppermute | solution.py:24
  110.2 8.5 %collective-permute-start.14 = (bf16[2,264,256]{2,1,0:T(8,128)(2,1)S(1)}, bf16[2,264,256]{2,1,0:T(8,128)(2,1)S(1)}, u32[]{:S(2)}, u32[]{:S(2)}) collective-permute-start(bf16[2,264,256]{2,1,0:T(8,128)(2,1)S(1)} %slice_bitcast_fusion), channel_id=1, source_target_pairs={{0,96},{32,0},{64,32},{96,64},{1,97},{33,1},{65,33},{97,65},{2,98}... | collective-permute-start | bytes 811016 | tf_op jit(solution)/shard_map/ppermute | solution.py:24
  112.9 6.9 %collective-permute-start.13 = (bf16[264,256]{1,0:T(8,128)(2,1)S(1)}, bf16[264,256]{1,0:T(8,128)(2,1)S(1)}, u32[]{:S(2)}, u32[]{:S(2)}) collective-permute-start(bf16[264,256]{1,0:T(8,128)(2,1)S(1)} %get-tuple-element.32), channel_id=1, source_target_pairs={{0,16},{16,0},{1,17},{17,1},{2,18},{18,2},{3,19},{19,3},{4,20},{20... | collective-permute-start | bytes 405512 | tf_op jit(solution)/shard_map/ppermute | solution.py:24
  113.7 6.1 %collective-permute-start.11 = (bf16[264,256]{1,0:T(8,128)(2,1)S(1)}, bf16[264,256]{1,0:T(8,128)(2,1)S(1)}, u32[]{:S(2)}, u32[]{:S(2)}) collective-permute-start(bf16[264,256]{1,0:T(8,128)(2,1)S(1)} %get-tuple-element.26), channel_id=1, source_target_pairs={{0,16},{16,0},{1,17},{17,1},{2,18},{18,2},{3,19},{19,3},{4,20},{20... | collective-permute-start | bytes 405512 | tf_op jit(solution)/shard_map/ppermute | solution.py:24
  118.7 2.1 %collective-permute-start.15 = (bf16[264,256]{1,0:T(8,128)(2,1)S(1)}, bf16[264,256]{1,0:T(8,128)(2,1)S(1)}, u32[]{:S(2)}, u32[]{:S(2)}) collective-permute-start(bf16[264,256]{1,0:T(8,128)(2,1)S(1)} %get-tuple-element.30), channel_id=1, source_target_pairs={{0,16},{16,0},{1,17},{17,1},{2,18},{18,2},{3,19},{19,3},{4,20},{20... | collective-permute-start | bytes 405512 | tf_op jit(solution)/shard_map/ppermute | solution.py:24
